TPU v7x, 128 devices: a whole 4x4x4 slice. The times are simulated.
128 devices in a mesh: row: 8 (over y_hi, x), col: 16 (over y_lo, z, core).
Axes of the slice: x: 4, y: 4 (y_hi: 2, y_lo: 2; y = y_hi * 2 + y_lo), z: 4, core: 2. Of those that a mesh axis runs over, the one named last changes fastest.
Arguments:
- slip_log: float32 [512, 32768], P(None, ('row', 'col')), may hold values from -2.5 to 2.5
- fault_state: float32 [512, 32768], P(None, ('row', 'col')), may hold values from -2.5 to 2.5
- direct_effect: float32 [512, 32768], P(None, ('row', 'col')), may hold values from 0.3 to 1
- loading: float32 [512, 32768], P(None, ('row', 'col')), may hold values from 0.5 to 1.5
- dense_near: bfloat16 [32, 3, 1024, 1024], P('row', None, 'col'), may hold values from -0.109375 to 0.109375
- low_left: bfloat16 [32, 32, 32, 1024], P('row', 'col'), may hold values from -1 to 1
- low_right: bfloat16 [32, 32, 32, 1024], P('row', 'col'), may hold values from -0.03125 to 0.03125
- block_ranks: int32 [32, 32], P('row', 'col'), may hold values from 8 to 32
Outputs:
- new_log: float32 [512, 32768], P(None, ('row', 'col'))
- new_state: float32 [512, 32768], P(None, ('row', 'col'))
Inputs may be any that keep to these rules, and one draw needn't show every extreme that they name: `block_ranks`: only factor pairs below this count take part in a far block; entries of near blocks are not read.
All inputs are finite; a program needn't handle non-finite values.
Results may differ from a plain program's by a relative error of at most 0.0016.
Values may be sent and summed in bfloat16 or wider, within the bound.
No kernel may reach another device: no remote copies, remote signals or barrier semaphores. Data moves between devices by JAX's collectives and lax.ppermute only.
A program may use at most 128 MiB of HBM per device.

v0:
```python
import jax
import jax.numpy as jnp
from jax import lax
from jax.sharding import PartitionSpec as P

step_length = 0.25
damping = 0.5


def from_root(value, axis, source):
    kept = jnp.where(lax.axis_index(axis) == source, value, 0).astype(value.dtype)
    return lax.psum(kept, axis)


def with_halo(array, sides, width):
    for axis, dim in sides:
        size, length = (lax.axis_size(axis), array.shape[dim])
        up = [(i, (i + 1) % size) for i in range(size)]
        down = [(j, i) for i, j in up]
        last = lax.slice_in_dim(array, length - width, length, axis=dim)
        leading = lax.slice_in_dim(array, 0, width, axis=dim)
        before = lax.ppermute(last, axis, up)
        after = lax.ppermute(leading, axis, down)
        array = jnp.concatenate([before, array, after], axis=dim)
    return array


def friction_rates(log_rate, state_var, effect, load, traction):
    velocity = jnp.exp(log_rate)
    state_rate = jnp.exp(-state_var) - velocity
    log_change = (load - traction - state_rate) / (effect + damping * velocity)
    return (log_change, state_rate)


def advance(section, log_now, state_now):
    first_log, first_state = section(log_now, state_now)
    mid_log = log_now + step_length * first_log
    mid_state = state_now + step_length * first_state
    second_log, second_state = section(mid_log, mid_state)
    new_log = log_now + 0.5 * step_length * (first_log + second_log)
    new_state = state_now + 0.5 * step_length * (first_state + second_state)
    return (new_log, new_state)


def on_device(
    slip_log, fault_state, direct_effect, loading, dense_near, low_left, low_right, block_ranks
):
    column = lax.axis_index("col")
    row_index = lax.axis_index("row")
    fanout = lax.axis_size("col") // lax.axis_size("row")
    source_row = column // fanout
    half_index = column % fanout
    members = slip_log.shape[0]
    row_blocks = low_right.shape[0]
    col_blocks = low_right.shape[1]
    leaf_size = low_right.shape[3]
    rows_sub = dense_near.shape[2]
    total_blocks = col_blocks * lax.axis_size("col")
    levels = jnp.arange(low_right.shape[2], dtype=jnp.int32)
    global_rows = row_index * row_blocks + jnp.arange(row_blocks, dtype=jnp.int32)
    global_cols = column * col_blocks + jnp.arange(col_blocks, dtype=jnp.int32)
    distance = jnp.abs(global_rows[:, None] - global_cols[None, :])
    far_mask = jnp.minimum(distance, total_blocks - distance) > 1
    keep = ((levels[None, None, :] < block_ranks[:, :, None]) & far_mask[:, :, None]).astype(
        jnp.float32
    )

    def spread(row_slip):
        width = row_slip.shape[1] // fanout
        chosen = lax.dynamic_slice_in_dim(row_slip, half_index * width, width, 1)
        return from_root(chosen, "row", source_row)

    def near_field(row_slip):
        blocked = row_slip.reshape(members, row_blocks, leaf_size)
        extended = with_halo(blocked, (("row", 1),), 1)
        window = jnp.stack([extended[:, :-2], extended[:, 1:-1], extended[:, 2:]], axis=2)
        near = jnp.einsum("erol,roil->eri", window, dense_near, preferred_element_type=jnp.float32)
        full = jnp.zeros((members, row_blocks, leaf_size), jnp.float32)
        full = lax.dynamic_update_slice_in_dim(full, near, column * rows_sub, 2)
        return full.reshape(members, -1)

    def operate(column_slip):
        columns = column_slip.reshape(members, col_blocks, leaf_size)
        coeffs = (
            jnp.einsum("ecj,rckj->erck", columns, low_right, preferred_element_type=jnp.float32)
            * keep[None]
        )
        far_sum = jnp.einsum(
            "erck,rcki->eri",
            coeffs.astype(jnp.bfloat16),
            low_left,
            preferred_element_type=jnp.float32,
        )
        return far_sum.reshape(members, -1)

    def section(log_rate, state_var):
        slip_bf = jnp.exp(log_rate).astype(jnp.bfloat16)
        row_slip = lax.all_gather(slip_bf, "col", axis=1, tiled=True)
        terms = operate(spread(row_slip)) + near_field(row_slip)
        traction = lax.psum_scatter(terms, "col", scatter_dimension=1, tiled=True)
        return friction_rates(log_rate, state_var, direct_effect, loading, traction)

    new_log, new_state = advance(section, slip_log, fault_state)
    return (new_log, new_state)


def solution(mesh):
    in_specs = (
        P(None, ("row", "col")),
        P(None, ("row", "col")),
        P(None, ("row", "col")),
        P(None, ("row", "col")),
        P("row", None, "col", None),
        P("row", "col", None, None),
        P("row", "col", None, None),
        P("row", "col"),
    )
    out_specs = (P(None, ("row", "col")), P(None, ("row", "col")))
    return jax.shard_map(
        on_device, mesh=mesh, in_specs=in_specs, out_specs=out_specs, check_vma=False
    )
```

profile of v0, /device:TPU:0, one launch (start us, length us, event | category | flops | bytes accessed | tf_op | source)
XLA Modules:
  0.0 514.8 jit_solution(16797406905524143720)
XLA Ops:
  9.5 40.7 %all-gather.3.cloned.1.call-done = bf16[512,4096]{0,1:T(8,128)(2,1)} async-done(((bf16[512,256]{0,1:T(8,128)(2,1)}), bf16[512,4096]{0,1:T(8,128)(2,1)}) %all-gather.3.cloned.1.call-update) | async-done | bytes 4194320 | tf_op jit(solution)/shard_map/all_gather | solution.py:98
  53.5 6.3 %copy.17 = bf16[512,4,1024]{2,0,1:T(8,128)(2,1)} copy(bf16[512,4,1024]{0,2,1:T(8,128)(2,1)} %bitcast.90) | data formatting | bytes 8388608 | tf_op jit(solution)/shard_map/reshape | solution.py:74
  64.4 4.2 collective-permute-start.1
  68.8 6.3 %copy.21 = bf16[512,4,1,1024]{3,0,2,1:T(8,128)(2,1)} copy(bf16[512,4,1,1024]{0,3,1,2:T(8,128)(2,1)} %bitcast.91) | data formatting | bytes 8388608 | tf_op jit(solution)/shard_map/stack;reshape | solution.py:76
  75.1 34.8 %collective-permute-done = bf16[512,1,1024]{2,0,1:T(8,128)(2,1)} collective-permute-done((bf16[512,1,1024]{2,0,1:T(8,128)(2,1)}, bf16[512,1,1024]{2,0,1:T(8,128)(2,1)}, u32[]{:S(2)}, u32[]{:S(2)}) %collective-permute-start) | collective-permute-done | bytes 1048608 | tf_op jit(solution)/shard_map/ppermute | solution.py:22
  109.9 5.8 %fusion.15 = (bf16[512,4,1,1024]{3,0,2,1:T(8,128)(2,1)}, bf16[512,4,1,1024]{3,0,2,1:T(8,128)(2,1)}) fusion(bf16[512,4,1024]{2,0,1:T(8,128)(2,1)} %copy.17, bf16[512,1,1024]{2,0,1:T(8,128)(2,1)} %collective-permute-done, bf16[512,1,1024]{2,0,1:T(8,128)(2,1)} %collective-permute-done.1), kind=kLoop, calls=%fused_computation.19 | loop fusion | flops 4194304 | bytes 14680064 | tf_op jit(solution)/shard_map/stack | solution.py:76
  115.6 38.6 %all-reduce.3.cloned.1.call-done = bf16[512,2,1024]{0,2,1:T(8,128)(2,1)} async-done(((bf16[512,2,1024]{0,2,1:T(8,128)(2,1)}), bf16[512,2,1024]{0,2,1:T(8,128)(2,1)}) %all-reduce.3.cloned.1.call-update) | async-done | bytes 2097168 | tf_op jit(solution)/shard_map/psum | solution.py:12
  154.3 6.5 %fusion.60 = f32[4,512,1024,1]{2,1,3,0:T(8,128)} fusion(bf16[4,2,32,1024]{3,2,1,0:T(8,128)(2,1)S(1)} %copy-done.2, bf16[4,2,32,1024]{3,2,1,0:T(8,128)(2,1)S(1)} %copy-done.3, bf16[512,2,1024]{0,2,1:T(8,128)(2,1)} %all-reduce.3.cloned.1.call-done, f32[4,2,32]{2,1,0:T(2,128)S(1)} %and_convert_fusion), kind=kOutput, calls=%fused_computation.39 | convolution fusion | flops 537133056 | bytes 11535360 | tf_op jit(solution)/shard_map/erck,rcki->eri/dot_general | solution.py:88
  160.8 6.7 %fusion.35 = f32[512,4,64]{2,0,1:T(8,128)S(1)} fusion(bf16[4,3,64,1024]{3,2,1,0:T(8,128)(2,1)S(1)} %copy-done, bf16[512,4,1,1024]{3,0,2,1:T(8,128)(2,1)} %get-tuple-element.11, bf16[512,4,1,1024]{3,0,2,1:T(8,128)(2,1)} %copy.21, bf16[512,4,1,1024]{3,0,2,1:T(8,128)(2,1)} %get-tuple-element.10, f32[4,512,1024]{2,1,0:T(8,128)} %bitcast.88, s32[]{:T(128)S(6)} %select_n.36), kind=kOutput, calls=%fused_computation.31 | convolution fusion | flops 818020352 | bytes 15204356 | tf_op jit(solution)/shard_map/erol,roil->eri/dot_general | solution.py:77
  167.5 5.8 %add.88 = f32[512,4,1024]{2,0,1:T(8,128)} dynamic-update-slice(f32[512,4,1024]{2,0,1:T(8,128)} %bitcast.89, f32[512,4,64]{2,0,1:T(8,128)S(1)} %fusion.35, s32[]{:T(128)} %constant.43.clone.1, s32[]{:T(128)} %constant.43.clone.1, s32[]{:T(128)S(6)} %select_n.36) | dynamic-update-slice | bytes 1048580 | tf_op jit(solution)/shard_map/add | solution.py:99
  173.2 8.7 %copy.23 = f32[512,4,1024]{0,2,1:T(8,128)} copy(f32[512,4,1024]{2,0,1:T(8,128)} %add.88) | data formatting | bytes 16777216 | tf_op jit(solution)/shard_map/add | solution.py:99
  186.5 69.6 %reduce-scatter.3.cloned.1.call-done = f32[512,256]{0,1:T(8,128)} async-done(((f32[512,4096]{0,1:T(8,128)}), f32[512,256]{0,1:T(8,128)}) %reduce-scatter.3.cloned.1.call-update) | async-done | bytes 524304 | tf_op jit(solution)/shard_map/reduce_scatter | solution.py:100
  260.0 35.8 %all-gather.5.cloned.1.call-done = bf16[512,4096]{0,1:T(8,128)(2,1)} async-done(((bf16[512,256]{0,1:T(8,128)(2,1)}), bf16[512,4096]{0,1:T(8,128)(2,1)}) %all-gather.5.cloned.1.call-update) | async-done | bytes 4194320 | tf_op jit(solution)/shard_map/all_gather | solution.py:98
  299.3 6.3 %copy.28 = bf16[512,4,1024]{2,0,1:T(8,128)(2,1)} copy(bf16[512,4,1024]{0,2,1:T(8,128)(2,1)} %bitcast.92) | data formatting | bytes 8388608 | tf_op jit(solution)/shard_map/reshape | solution.py:74
  310.1 4.2 collective-permute-start.3
  314.3 6.3 %copy.32 = bf16[512,4,1,1024]{3,0,2,1:T(8,128)(2,1)} copy(bf16[512,4,1,1024]{0,3,1,2:T(8,128)(2,1)} %bitcast.93) | data formatting | bytes 8388608 | tf_op jit(solution)/shard_map/stack;reshape | solution.py:76
  320.6 35.0 %collective-permute-done.2 = bf16[512,1,1024]{2,0,1:T(8,128)(2,1)} collective-permute-done((bf16[512,1,1024]{2,0,1:T(8,128)(2,1)}, bf16[512,1,1024]{2,0,1:T(8,128)(2,1)}, u32[]{:S(2)}, u32[]{:S(2)}) %collective-permute-start.2) | collective-permute-done | bytes 1048608 | tf_op jit(solution)/shard_map/ppermute | solution.py:22
  355.6 5.8 %fusion.13 = (bf16[512,4,1,1024]{3,0,2,1:T(8,128)(2,1)}, bf16[512,4,1,1024]{3,0,2,1:T(8,128)(2,1)}) fusion(bf16[512,4,1024]{2,0,1:T(8,128)(2,1)} %copy.28, bf16[512,1,1024]{2,0,1:T(8,128)(2,1)} %collective-permute-done.2, bf16[512,1,1024]{2,0,1:T(8,128)(2,1)} %collective-permute-done.3), kind=kLoop, calls=%fused_computation.15 | loop fusion | flops 4194304 | bytes 14680064 | tf_op jit(solution)/shard_map/stack | solution.py:76
  361.4 38.6 %all-reduce.5.cloned.1.call-done = bf16[512,2,1024]{0,2,1:T(8,128)(2,1)} async-done(((bf16[512,2,1024]{0,2,1:T(8,128)(2,1)}), bf16[512,2,1024]{0,2,1:T(8,128)(2,1)}) %all-reduce.5.cloned.1.call-update) | async-done | bytes 2097168 | tf_op jit(solution)/shard_map/psum | solution.py:12
  399.9 6.8 %fusion.57 = f32[4,512,1024,1]{2,1,3,0:T(8,128)} fusion(bf16[4,2,32,1024]{3,2,1,0:T(8,128)(2,1)} %param.13, bf16[4,2,32,1024]{3,2,1,0:T(8,128)(2,1)} %param.14, bf16[512,2,1024]{0,2,1:T(8,128)(2,1)} %all-reduce.5.cloned.1.call-done, f32[4,2,32]{2,1,0:T(2,128)S(1)} %and_convert_fusion), kind=kOutput, calls=%fused_computation.38 | convolution fusion | flops 537133056 | bytes 11535360 | tf_op jit(solution)/shard_map/erck,rcki->eri/dot_general | solution.py:88
  406.7 7.4 %fusion.26 = f32[512,4,64]{2,0,1:T(8,128)} fusion(bf16[4,3,64,1024]{3,2,1,0:T(8,128)(2,1)S(1)} %copy-done, bf16[512,4,1,1024]{3,0,2,1:T(8,128)(2,1)} %get-tuple-element.7, bf16[512,4,1,1024]{3,0,2,1:T(8,128)(2,1)} %copy.32, bf16[512,4,1,1024]{3,0,2,1:T(8,128)(2,1)} %get-tuple-element.6, f32[4,512,1024]{2,1,0:T(8,128)} %bitcast.86, s32[]{:T(128)S(6)} %select_n.36), kind=kOutput, calls=%fused_computation.28 | convolution fusion | flops 818020352 | bytes 15204356 | tf_op jit(solution)/shard_map/erol,roil->eri/dot_general | solution.py:77
  414.2 6.1 %add.92 = f32[512,4,1024]{2,0,1:T(8,128)} dynamic-update-slice(f32[512,4,1024]{2,0,1:T(8,128)} %bitcast.87, f32[512,4,64]{2,0,1:T(8,128)} %fusion.26, s32[]{:T(128)} %constant.43.clone.1, s32[]{:T(128)} %constant.43.clone.1, s32[]{:T(128)S(6)} %select_n.36) | dynamic-update-slice | bytes 1048580 | tf_op jit(solution)/shard_map/add | solution.py:99
  420.3 8.7 %copy.34 = f32[512,4,1024]{0,2,1:T(8,128)} copy(f32[512,4,1024]{2,0,1:T(8,128)} %add.92) | data formatting | bytes 16777216 | tf_op jit(solution)/shard_map/add | solution.py:99
  431.1 72.0 %reduce-scatter.5.cloned.1.call-done = f32[512,256]{0,1:T(8,128)} async-done(((f32[512,4096]{0,1:T(8,128)}), f32[512,256]{0,1:T(8,128)}) %reduce-scatter.5.cloned.1.call-update) | async-done | bytes 524304 | tf_op jit(solution)/shard_map/reduce_scatter | solution.py:100
  (47 shorter events, 33.6 us)
Async XLA Ops:
  7.2 153.6 %copy-start = (bf16[4,3,64,1024]{3,2,1,0:T(8,128)(2,1)S(1)}, bf16[4,3,64,1024]{3,2,1,0:T(8,128)(2,1)}, u32[]{:S(2)}) copy-start(bf16[4,3,64,1024]{3,2,1,0:T(8,128)(2,1)} %param.12) | copy-start | bytes 4718596
  7.2 43.0 %all-gather.3.cloned.1.call-start = ((), (), s32[]{:S(2)}) async-start(), calls=%async_computation.2 | async-start | bytes 4456448 | tf_op jit(solution)/shard_map/all_gather | solution.py:98
  9.4 144.9 %all-reduce.3.cloned.1.call-start = ((), (), s32[]{:S(2)}) async-start(), calls=%async_computation.3 | async-start | bytes 4194304 | tf_op jit(solution)/shard_map/psum | solution.py:12
  53.5 202.6 %reduce-scatter.3.cloned.1.call-start = ((), (), s32[]{:S(2)}) async-start(), calls=%async_computation.4 | async-start | bytes 8912896 | tf_op jit(solution)/shard_map/reduce_scatter | solution.py:100
  59.8 8.7 %copy-start.5 = (s32[4,2]{0,1:T(2,128)S(1)}, s32[4,2]{0,1:T(2,128)}, u32[]{:S(2)}) copy-start(s32[4,2]{0,1:T(2,128)} %param.15) | copy-start | bytes 100
  62.9 47.0 %collective-permute-start = (bf16[512,1,1024]{2,0,1:T(8,128)(2,1)}, bf16[512,1,1024]{2,0,1:T(8,128)(2,1)}, u32[]{:S(2)}, u32[]{:S(2)}) collective-permute-start(bf16[512,1,1024]{2,0,1:T(8,128)(2,1)} %get-tuple-element.12), channel_id=1, source_target_pairs={{0,16},{16,32},{32,48},{48,64},{64,80},{80,96},{96,112},{112,0},{1... | collective-permute-start | bytes 3145736 | tf_op jit(solution)/shard_map/ppermute | solution.py:22
  64.4 45.5 %collective-permute-start.1 = (bf16[512,1,1024]{2,0,1:T(8,128)(2,1)}, bf16[512,1,1024]{2,0,1:T(8,128)(2,1)}, u32[]{:S(2)}, u32[]{:S(2)}) collective-permute-start(bf16[512,1,1024]{2,0,1:T(8,128)(2,1)} %get-tuple-element.13), channel_id=1, source_target_pairs={{16,0},{32,16},{48,32},{64,48},{80,64},{96,80},{112,96},{0,112},{1... | collective-permute-start | bytes 3145736 | tf_op jit(solution)/shard_map/ppermute | solution.py:23
  75.1 79.1 %copy-start.2 = (bf16[4,2,32,1024]{3,2,1,0:T(8,128)(2,1)S(1)}, bf16[4,2,32,1024]{3,2,1,0:T(8,128)(2,1)}, u32[]{:S(2)}) copy-start(bf16[4,2,32,1024]{3,2,1,0:T(8,128)(2,1)} %param.13) | copy-start | bytes 1572868
  75.1 79.1 %copy-start.3 = (bf16[4,2,32,1024]{3,2,1,0:T(8,128)(2,1)S(1)}, bf16[4,2,32,1024]{3,2,1,0:T(8,128)(2,1)}, u32[]{:S(2)}) copy-start(bf16[4,2,32,1024]{3,2,1,0:T(8,128)(2,1)} %param.14) | copy-start | bytes 1572868
  181.9 1.0 copy-start.4
  182.0 113.9 %all-gather.5.cloned.1.call-start = ((), (), s32[]{:S(2)}) async-start(), calls=%async_computation.5 | async-start | bytes 4456448 | tf_op jit(solution)/shard_map/all_gather | solution.py:98
  258.5 0.8 copy-start.1
  260.0 139.9 %all-reduce.5.cloned.1.call-start = ((), (), s32[]{:S(2)}) async-start(), calls=%async_computation.6 | async-start | bytes 4194304 | tf_op jit(solution)/shard_map/psum | solution.py:12
  299.2 203.9 %reduce-scatter.5.cloned.1.call-start = ((), (), s32[]{:S(2)}) async-start(), calls=%async_computation.7 | async-start | bytes 8912896 | tf_op jit(solution)/shard_map/reduce_scatter | solution.py:100
  308.6 47.0 %collective-permute-start.2 = (bf16[512,1,1024]{2,0,1:T(8,128)(2,1)}, bf16[512,1,1024]{2,0,1:T(8,128)(2,1)}, u32[]{:S(2)}, u32[]{:S(2)}) collective-permute-start(bf16[512,1,1024]{2,0,1:T(8,128)(2,1)} %get-tuple-element.8), channel_id=1, source_target_pairs={{0,16},{16,32},{32,48},{48,64},{64,80},{80,96},{96,112},{112,0},{1... | collective-permute-start | bytes 3145736 | tf_op jit(solution)/shard_map/ppermute | solution.py:22
  310.1 45.5 %collective-permute-start.3 = (bf16[512,1,1024]{2,0,1:T(8,128)(2,1)}, bf16[512,1,1024]{2,0,1:T(8,128)(2,1)}, u32[]{:S(2)}, u32[]{:S(2)}) collective-permute-start(bf16[512,1,1024]{2,0,1:T(8,128)(2,1)} %get-tuple-element.9), channel_id=1, source_target_pairs={{16,0},{32,16},{48,32},{64,48},{80,64},{96,80},{112,96},{0,112},{1... | collective-permute-start | bytes 3145736 | tf_op jit(solution)/shard_map/ppermute | solution.py:23
Sparse Core Ops, SparseCore 0:
  10.3 39.8 all-gather.2
  53.6 100.5 all-reduce.2
  182.1 73.9 reduce-scatter.2
  260.1 35.7 all-gather.4
  299.4 100.5 all-reduce.4
  429.1 73.9 reduce-scatter.4
where the time goes:
time: 516 us; the launch traced here: 515 us
  waiting for transfers between devices  365 us (71%)
  local copies, waits for them, and re-layouts  71.4 us (14%)
  matrix products  27.4 us (5%)
  other arithmetic  25 us (5%)
  between operations  14.2 us (3%)
  starting transfers between devices  11.5 us (2%)
    reduce_scatter x2, waiting for transfers between devices, section(): traction = lax.psum_scatter(terms, 'col', scatter_dimension=1, tiled=True)  142 us
    psum x2, waiting for transfers between devices, from_root(): return lax.psum(kept, axis)  77.2 us
    all_gather x2, waiting for transfers between devices, section(): row_slip = lax.all_gather(slip_bf, 'col', axis=1, tiled=True)  76.5 us
    ppermute x2, waiting for transfers between devices, with_halo(): before = lax.ppermute(last, axis, up)  69.8 us
    add x4, local copies, waits for them, and re-layouts, section(): terms = operate(spread(row_slip)) + near_field(row_slip)  29.3 us
    dot_general x2, matrix products, near_field(): jnp.einsum('erol,roil->eri', window, dense_near, preferred_element_type=j...  14.1 us
    dot_general x2, matrix products, operate(): jnp.einsum('erck,rcki->eri', coeffs.astype(jnp.bfloat16), low_left, prefe...  13.3 us
    reshape x2, local copies, waits for them, and re-layouts, near_field(): blocked = row_slip.reshape(members, row_blocks, leaf_size)  12.6 us
  transfers between devices with their start and end apart: 10, of which 8 were waited for; matrix products, arithmetic and copies ran while one was open for 9% of the time, Pallas kernels for 0%

commit v1 on v0

v1 whole, which is shorter than its diff:
```python
import functools
import jax
import jax.numpy as jnp
from jax import lax
from jax.experimental import pallas as pl
from jax.experimental.pallas import tpu as pltpu
from jax.sharding import Mesh, PartitionSpec as P

step_length = 0.25
damping = 0.5
ALL = ("row", "chip", "core")
F32 = jnp.float32
BF16 = jnp.bfloat16
COUNT = 128


def pick(array, index, axis=0):
    return lax.dynamic_index_in_dim(array, index, axis, keepdims=False)


def move(value, target):
    return lax.ppermute(value, ALL, [(d, target(d)) for d in range(COUNT)])


def dot(a, b):
    return jnp.dot(a, b, preferred_element_type=F32)


def shape(*dims, dtype=F32):
    return jax.ShapeDtypeStruct(dims, dtype)


STATE = shape(512, 256)
SLIP = shape(512, 256, dtype=BF16)
TURNED = shape(256, 256)
HALF = shape(256, 256, dtype=BF16)
LEFT = shape(512, 1024, dtype=BF16)
SENT = shape(32, 2, 16, 256, dtype=BF16)
RIGHT = shape(512, 1024, dtype=BF16)
NEAR = shape(3, 512, 1024, dtype=BF16)
SCALARS = pl.BlockSpec(memory_space=pltpu.SMEM)
VECTORS = pl.BlockSpec(memory_space=pltpu.VMEM)


def call(kernel, outs, where, operands, flops, scratch=()):
    return pl.pallas_call(
        kernel,
        out_shape=outs,
        in_specs=[SCALARS] + [VECTORS] * len(operands),
        out_specs=[VECTORS] * len(outs),
        scratch_shapes=scratch,
        cost_estimate=pl.CostEstimate(flops=flops, bytes_accessed=5 << 20, transcendentals=0),
    )(where, *operands)


def coefficients_of(right_ref, own, pair, out_ref):
    total = dot(right_ref[:, :512], own[...]) + dot(right_ref[:, 512:], pair[...])
    blocks = total.astype(BF16).reshape(32, 16, 256)
    out_ref[:, 0] = blocks
    out_ref[:, 1] = blocks


def coeff_kernel(where_ref, right_ref, own, pair, out_ref):
    coefficients_of(right_ref, own, pair, out_ref)


def coeff_first_kernel(where_ref, *refs):
    parts, own, pair, out_ref, right_ref = refs[:8], *refs[8:]
    quarter, core, x_at = where_ref[0], where_ref[1], where_ref[3]
    for b in range(2):
        for u in range(4):
            r = (b ^ core) * 4 + (u ^ x_at)
            for t in range(4):
                start = pl.multiple_of((quarter ^ t) * 256, 256)
                right_ref[pl.ds(pl.multiple_of(r * 64, 64), 64), t * 256 : t * 256 + 256] = parts[b * 4 + u][
                    :, pl.ds(start, 256)
                ]
    coefficients_of(right_ref, own, pair, out_ref)


def near_inner(pieces, near_ref, out_ref):
    own, pair, inner, outer = pieces
    total = dot(near_ref[1, :, :512], own[...]) + dot(near_ref[1, :, 512:], pair[...])
    total = total + dot(near_ref[0, :, 512:], inner[...])
    out_ref[...] = total + dot(near_ref[2, :, 512:], outer[...])


def near_first_kernel(where_ref, *refs):
    pieces, parts, num, (out_ref, near_ref) = refs[:6], refs[6:14], refs[14], refs[15:]
    quarter, block, odd = where_ref[0], where_ref[2], where_ref[4]
    for half in range(2):
        for s in range(4):
            rows = pl.ds(pl.multiple_of(half * 256 + (block ^ s) * 64, 64), 64)
            for side, o in enumerate((2 - 2 * odd, 1, 2 * odd)):
                for t in range(4):
                    start = pl.multiple_of((quarter ^ t) * 256, 256)
                    near_ref[side, rows, t * 256 : t * 256 + 256] = parts[half * 4 + s][o, :, pl.ds(start, 256)]
    own, pair, inner, outer, across, beyond = pieces
    total = None
    for side, (low, high) in enumerate(((across, inner), (own, pair), (beyond, outer))):
        term = dot(near_ref[side, :, :512], low[...]) + dot(near_ref[side, :, 512:], high[...])
        total = term if total is None else total + term
    out_ref[...] = num[...] - total


def near_kernel(where_ref, own, pair, inner, outer, near_ref, out_ref):
    near_inner((own, pair, inner, outer), near_ref, out_ref)


def left_kernel(where_ref, own, received, out_ref):
    out_ref[:256] = own[...].T
    out_ref[256:] = received[...].T


def raise_kernel(where_ref, log, own, theirs):
    own[...] = jnp.exp(log[pl.ds(pl.multiple_of(where_ref[1] * 256, 256), 256), :]).astype(BF16)
    theirs[...] = jnp.exp(log[pl.ds(pl.multiple_of(256 - where_ref[1] * 256, 256), 256), :]).astype(BF16)


def join_kernel(where_ref, own, received, out_ref):
    out_ref[:256] = own[...].T
    out_ref[256:] = received[...].T


def prepare_first_kernel(where_ref, *refs):
    whole, received, (log_ref, effect_ref, load_ref, num, den, mid_state, sum_state) = refs[:4], refs[4:8], refs[8:]
    mine = pl.ds(pl.multiple_of(where_ref[1] * 256, 256), 256)
    for half in range(2):
        rows = slice(half * 256, half * 256 + 256)
        log, state, effect, load = (
            (received[i][...] if half else whole[i][mine, :]).T for i in range(4)
        )
        velocity = jnp.exp(log)
        state_rate = jnp.exp(-state) - velocity
        log_ref[rows] = log
        effect_ref[rows] = effect
        load_ref[rows] = load
        num[rows] = load - state_rate
        den[rows] = effect + damping * velocity
        mid_state[rows] = state + step_length * state_rate
        sum_state[rows] = state + 0.5 * step_length * state_rate


def prepare_second_kernel(where_ref, log, state, effect, load, sum_state, num, den, own, other):
    place = pl.ds(pl.multiple_of(where_ref[1] * 256, 256), 256)
    for half in range(2):
        rows = slice(half * 256, half * 256 + 256)
        velocity = jnp.exp(log[rows])
        state_rate = jnp.exp(-state[rows]) - velocity
        num[rows] = load[rows] - state_rate
        den[rows] = effect[rows] + damping * velocity
        new_state = (sum_state[rows] + 0.5 * step_length * state_rate).T
        if half:
            other[...] = new_state
        else:
            own[place, :] = new_state


def near_outer_kernel(where_ref, num, partial, across, beyond, near_ref, out_ref):
    near = partial[...] + dot(near_ref[0, :, :512], across[...]) + dot(near_ref[2, :, :512], beyond[...])
    out_ref[...] = num[...] - near


def far_first_kernel(where_ref, coeff, left, num, den, log, mid_log, sum_log, slip):
    for half in range(2):
        rows = slice(half * 256, half * 256 + 256)
        change = (num[rows] - dot(left[rows], coeff[...])) / den[rows]
        middle = log[rows] + step_length * change
        mid_log[rows] = middle
        sum_log[rows] = log[rows] + 0.5 * step_length * change
        slip[rows] = jnp.exp(middle).astype(BF16)


def far_second_kernel(where_ref, coeff, left, num, den, sum_log, own, other):
    place = pl.ds(pl.multiple_of(where_ref[1] * 256, 256), 256)
    for half in (1, 0):
        rows = slice(half * 256, half * 256 + 256)
        change = (num[rows] - dot(left[rows], coeff[...])) / den[rows]
        result = (sum_log[rows] + 0.5 * step_length * change).T
        if half:
            other[...] = result
        else:
            own[place, :] = result


def on_device(
    slip_log, fault_state, direct_effect, loading, dense_near, low_left, low_right, block_ranks
):
    row, chip, core = (lax.axis_index(name) for name in ALL)
    col = chip * 2 + core
    block, quarter = col // 4, col % 4
    x_at, z_at = row % 4, chip % 4
    where = jnp.stack([quarter, core, block, x_at, block % 2]).astype(jnp.int32)
    partner = lambda d: d ^ 1
    zl = lambda d: d ^ 2

    fourths = low_right.reshape(4, 4, 16, 1024)
    along = [pick(fourths, z_at ^ t, 1) for t in range(4)]
    along = [along[0]] + [move(along[t], lambda d: d ^ (2 * t)) for t in range(1, 4)]

    def right_target(d, u):
        r, c = d // 16, d % 16
        return ((c // 8) * 4 + ((r % 4) ^ u)) * 16 + (c % 2) * 8 + (c // 2 % 4) * 2 + r // 4

    arrived = [
        move(lax.select_n(z_at ^ x_at ^ u, *along), functools.partial(right_target, u=u)).reshape(64, 1024)
        for u in range(4)
    ]
    right_parts = arrived + [move(arrived[u], partner) for u in range(4)]

    levels = jnp.arange(32, dtype=jnp.int32)
    rows_of = row * 4 + jnp.arange(4, dtype=jnp.int32)
    cols_of = col * 2 + jnp.arange(2, dtype=jnp.int32)
    distance = jnp.abs(rows_of[:, None] - cols_of[None, :])
    far = jnp.minimum(distance, 32 - distance) > 1
    keep = ((levels < block_ranks[:, :, None]) & far[:, :, None]).reshape(4, 1, 64, 1)
    left_out = low_left.reshape(4, 64, 4, 256).transpose(0, 2, 1, 3)
    left_out = jnp.where(keep, left_out, 0).astype(BF16).reshape(16, 64, 256)
    left = lax.all_to_all(left_out, ("chip", "core"), 0, 0).reshape(1024, 256)
    lefts = (left, move(left, partner))

    def near_target(d, s):
        r, a, q = d // 16, (d % 16) // 4, d % 4
        return r * 16 + (q ^ s) * 4 + a

    parts = [move(pick(dense_near, quarter ^ s), functools.partial(near_target, s=s)) for s in range(4)]
    parts = parts + [move(parts[s], partner) for s in range(4)]

    own, theirs = call(raise_kernel, [HALF, HALF], where, (slip_log,), 1)
    (slip,) = call(join_kernel, [SLIP], where, (own, move(theirs, partner)), 1)
    arrays = (slip_log, fault_state, direct_effect, loading)
    received = [move(lax.dynamic_slice_in_dim(v, (1 - core) * 256, 256, 0), partner) for v in arrays]

    def exchange(slip):
        pair = move(slip, zl)
        inner = move(slip, lambda d: d ^ 6)
        outer = move(slip, lambda d: ((d + 4 if d & 4 else d - 4) % COUNT) ^ 2)
        return (slip, pair, inner, outer), (move(pair, lambda d: d ^ 6), move(outer, zl))

    def all_to_all(sent):
        return lax.all_to_all(sent.reshape(64, 16, 256), ("row", "chip"), 0, 0).reshape(1024, 256)

    def restored(own, other):
        return lax.dynamic_update_slice(own, move(other, partner), ((1 - core) * 256, 0))

    pieces, crossed = exchange(slip)
    sent, right = call(coeff_first_kernel, [SENT, RIGHT], where, (*right_parts, *pieces[:2]), 1 << 28)
    coeff = all_to_all(sent)
    (left,) = call(left_kernel, [LEFT], where, lefts, 1 << 20)
    log, effect, load, num, den, mid_state, sum_state = call(
        prepare_first_kernel, [STATE] * 7, where, (*arrays, *received), 1
    )
    num, near = call(near_first_kernel, [STATE, NEAR], where, (*pieces, *crossed, *parts, num), 3 << 28)
    mid_log, sum_log, slip = call(far_first_kernel, [STATE, STATE, SLIP], where, (coeff, left, num, den, log), 1 << 28)

    pieces, crossed = exchange(slip)
    (sent,) = call(coeff_kernel, [SENT], where, (right, *pieces[:2]), 1 << 28)
    coeff = all_to_all(sent)
    (partial,) = call(near_kernel, [STATE], where, (*pieces, near), 2 << 28)
    num, den, own, other = call(
        prepare_second_kernel, [STATE, STATE, STATE, TURNED], where,
        (mid_log, mid_state, effect, load, sum_state), 1,
    )
    (num,) = call(near_outer_kernel, [STATE], where, (num, partial, *crossed, near), 1 << 28)
    new_state = restored(own, other)
    own, other = call(far_second_kernel, [STATE, TURNED], where, (coeff, left, num, den, sum_log), 1 << 28)
    return restored(own, other), new_state


def solution(mesh):
    chips = Mesh(mesh.devices.reshape(8, 8, 2), ALL)
    cells, columns = P(None, ALL), ("chip", "core")
    in_specs = (
        cells, cells, cells, cells,
        P("row", None, columns, None), P("row", columns, None, None), P("row", columns, None, None), P("row", columns),
    )
    return jax.shard_map(
        on_device, mesh=chips, in_specs=in_specs, out_specs=(cells, cells), check_vma=False
    )
```

time: 516 us -> 157 us (0.30)
  waiting for transfers between devices: 365 us -> 36.4 us
  local copies, waits for them, and re-layouts: 71.4 us -> 15.1 us
  starting transfers between devices: 11.5 us -> 62.7 us
  Pallas kernels: 0 us -> 37.7 us
  matrix products: 27.4 us -> 0 us
  other arithmetic: 25 us -> 2.53 us
  between operations: 14.2 us -> 1.05 us
    reduce_scatter x2 -> x0, waiting for transfers between devices: 142 us -> none  [section(): traction = lax.psum_scatter(terms, 'col', scatter_dimension=1, tiled=True)]
    psum x2 -> x0, waiting for transfers between devices: 77.2 us -> none  [from_root(): return lax.psum(kept, axis)]
    all_gather x2 -> x0, waiting for transfers between devices: 76.5 us -> none  [section(): row_slip = lax.all_gather(slip_bf, 'col', axis=1, tiled=True)]
    pallas_call x0 -> x12, Pallas kernels: none -> 37.7 us  [call(): pl.pallas_call(kernel, out_shape=outs, in_specs=[SCALARS] + [VECTORS] * l...]
    ppermute x4 -> x37, waiting for transfers between devices: 69.8 us -> 36.4 us  [move(): return lax.ppermute(value, ALL, [(d, target(d)) for d in range(COUNT)])]
    ppermute x4 -> x37, starting transfers between devices: 11.3 us -> 42.2 us  [move(): return lax.ppermute(value, ALL, [(d, target(d)) for d in range(COUNT)])]
    add x4 -> x0, local copies, waits for them, and re-layouts: 29.3 us -> none  [section(): terms = operate(spread(row_slip)) + near_field(row_slip)]
    dot_general x4 -> x0, matrix products: 27.4 us -> none  [the longest x2 14.1 us: near_field(): jnp.einsum('erol,roil->eri', window, dense_near, preferred_element_type=j...]
  transfers between devices with their start and end apart: 10 -> 40, of which waited for: 8 -> 10; matrix products, arithmetic and copies ran while one was open for 9% -> 7% of each run, Pallas kernels for 0% -> 22%
where the time goes in v1:
time: 157 us; the launch traced here: 155 us
  starting transfers between devices  62.7 us (40%)
  Pallas kernels  37.7 us (24%)
  waiting for transfers between devices  36.4 us (23%)
  local copies, waits for them, and re-layouts  15.1 us (10%)
  other arithmetic  2.53 us (2%)
    ppermute x37, starting transfers between devices, move(): return lax.ppermute(value, ALL, [(d, target(d)) for d in range(COUNT)])  42.2 us
    pallas_call x12, Pallas kernels, call(): pl.pallas_call(kernel, out_shape=outs, in_specs=[SCALARS] + [VECTORS] * l...  37.7 us
    ppermute x37, waiting for transfers between devices, move(): return lax.ppermute(value, ALL, [(d, target(d)) for d in range(COUNT)])  36.4 us
    all_to_all x2, starting transfers between devices, all_to_all(): lax.all_to_all(sent.reshape(64, 16, 256), ('row', 'chip'), 0, 0)  13.6 us
    all_to_all x1, starting transfers between devices, on_device(): left = lax.all_to_all(left_out, ('chip', 'core'), 0, 0).reshape(1024, 256)  6.82 us
    unnamed x69, local copies, waits for them, and re-layouts  5.63 us
    dynamic_slice x4, local copies, waits for them, and re-layouts, on_device(): lax.dynamic_slice_in_dim(v, (1 - core) * 256, 256, 0)  3.53 us
  transfers between devices with their start and end apart: 40, of which 10 were waited for; matrix products, arithmetic and copies ran while one was open for 7% of the time, Pallas kernels for 22%

profile of v1, /device:TPU:0, one launch (start us, length us, event | category | flops | bytes accessed | tf_op | source)
XLA Modules:
  0.0 155.5 jit_solution(7778790521305232981)
XLA Ops:
  7.2 3.6 %collective-permute-start.1 = (bf16[4,16,1024]{2,1,0:T(8,128)(2,1)}, bf16[4,16,1024]{2,1,0:T(8,128)(2,1)}, u32[]{:S(2)}, u32[]{:S(2)}) collective-permute-start(bf16[4,16,1024]{2,1,0:T(8,128)(2,1)} %get-tuple-element.55), channel_id=1, source_target_pairs={{0,4},{1,5},{2,6},{3,7},{4,0},{5,1},{6,2},{7,3},{8,12},{9,13},{10,... | collective-permute-start | bytes 393224 | tf_op jit(solution)/shard_map/ppermute | solution.py:22
  21.5 2.8 %collective-permute-start.6 = (bf16[4,16,1024]{2,1,0:T(8,128)(2,1)}, bf16[4,16,1024]{2,1,0:T(8,128)(2,1)S(1)}, u32[]{:S(2)}, u32[]{:S(2)}) collective-permute-start(bf16[4,16,1024]{2,1,0:T(8,128)(2,1)} %get-tuple-element.50), channel_id=1, source_target_pairs={{0,48},{1,56},{2,50},{3,58},{4,52},{5,60},{6,54},{7,62},{8,112},{9... | collective-permute-start | bytes 393224 | tf_op jit(solution)/shard_map/ppermute | solution.py:22
  31.3 5.3 %collective-permute-start.12 = (bf16[512,256]{1,0:T(8,128)(2,1)}, bf16[512,256]{1,0:T(8,128)(2,1)S(1)}, u32[]{:S(2)}, u32[]{:S(2)}) collective-permute-start(bf16[512,256]{1,0:T(8,128)(2,1)} %shard_map.96.refs_8_.refs_0_), channel_id=1, source_target_pairs={{0,2},{1,3},{2,0},{3,1},{4,6},{5,7},{6,4},{7,5},{8,10},{9,11},{10,... | collective-permute-start | bytes 786440 | tf_op jit(solution)/shard_map/ppermute | solution.py:22
  41.0 6.8 %all-to-all-start.1 = ((bf16[16,64,256]{2,1,0:T(8,128)(2,1)}), bf16[16,64,256]{2,1,0:T(8,128)(2,1)S(1)}, u32[]{:S(2)}, u32[]{:S(2)}) async-start(bf16[16,64,256]{2,1,0:T(8,128)(2,1)} %bitcast.17), calls=%async_computation.1 | async-start | bytes 1048576 | tf_op jit(solution)/shard_map/all_to_all | solution.py:219
  48.8 2.7 %collective-permute-done.15.refs_3_ = bf16[512,256]{1,0:T(8,128)(2,1)} collective-permute-done((bf16[512,256]{1,0:T(8,128)(2,1)}, bf16[512,256]{1,0:T(8,128)(2,1)}, u32[]{:S(2)}, u32[]{:S(2)}) %collective-permute-start.15) | collective-permute-done | bytes 262176 | tf_op jit(solution)/shard_map/ppermute | solution.py:22
  51.6 9.7 %collective-permute-done.14.refs_2_ = bf16[512,256]{1,0:T(8,128)(2,1)S(1)} collective-permute-done((bf16[512,256]{1,0:T(8,128)(2,1)}, bf16[512,256]{1,0:T(8,128)(2,1)S(1)}, u32[]{:S(2)}, u32[]{:S(2)}) %collective-permute-start.14) | collective-permute-done | bytes 262176 | tf_op jit(solution)/shard_map/ppermute | solution.py:22
  64.0 2.6 %collective-permute-start.16 = (bf16[512,256]{1,0:T(8,128)(2,1)S(1)}, bf16[512,256]{1,0:T(8,128)(2,1)}, u32[]{:S(2)}, u32[]{:S(2)}) collective-permute-start(bf16[512,256]{1,0:T(8,128)(2,1)S(1)} %collective-permute-done.12.refs_9_.refs_1_), channel_id=1, source_target_pairs={{0,6},{1,7},{2,4},{3,5},{4,2},{5,3},{6,0},{7,1},{8,14},{9,15},{10,... | collective-permute-start | bytes 786440 | tf_op jit(solution)/shard_map/ppermute | solution.py:22
  66.6 3.8 %collective-permute-done.19.refs_7_ = bf16[3,64,1024]{2,1,0:T(8,128)(2,1)S(1)} collective-permute-done((bf16[3,64,1024]{2,1,0:T(8,128)(2,1)S(1)}, bf16[3,64,1024]{2,1,0:T(8,128)(2,1)S(1)}, u32[]{:S(2)}, u32[]{:S(2)}) %collective-permute-start.19) | collective-permute-done | bytes 393248 | tf_op jit(solution)/shard_map/ppermute | solution.py:22
  70.5 4.9 %collective-permute-start.13 = (bf16[1024,256]{1,0:T(8,128)(2,1)S(1)}, bf16[1024,256]{1,0:T(8,128)(2,1)S(1)}, u32[]{:S(2)}, u32[]{:S(2)}) collective-permute-start(bf16[1024,256]{1,0:T(8,128)(2,1)S(1)} %bitcast.47), channel_id=1, source_target_pairs={{0,1},{1,0},{2,3},{3,2},{4,5},{5,4},{6,7},{7,6},{8,9},{9,8},{10,11... | collective-permute-start | bytes 1572872 | tf_op jit(solution)/shard_map/ppermute | solution.py:22
  75.4 2.8 %shard_map.97 = (bf16[32,2,16,256]{3,2,1,0:T(8,128)(2,1)}, bf16[512,1024]{1,0:T(8,128)(2,1)}) custom-call(s32[5]{0:T(128)} %stack.23.where_ref, bf16[64,1024]{1,0:T(8,128)(2,1)} %bitcast.10.refs_0_, bf16[64,1024]{1,0:T(8,128)(2,1)} %bitcast.11.refs_1_, bf16[64,1024]{1,0:T(8,128)(2,1)} %bitcast.58, bf16[64,1024]{1,0:T(8,128)(2,1)} %bitcast.56, ...), custom_call_target="tpu_custom_call" | custom-call | flops 268435456 | bytes 5242880 | tf_op jit(solution)/shard_map/pallas_call | solution.py:46
  78.2 5.4 %all-to-all-start = ((bf16[64,16,256]{2,1,0:T(8,128)(2,1)}), bf16[64,16,256]{2,1,0:T(8,128)(2,1)S(1)}, u32[]{:S(2)}, u32[]{:S(2)}) async-start(bf16[64,16,256]{2,1,0:T(8,128)(2,1)} %bitcast.52), calls=%async_computation | async-start | bytes 1048576 | tf_op jit(solution)/shard_map/all_to_all | solution.py:241
  87.2 4.1 %shard_map.99 = (f32[512,256]{1,0:T(8,128)}, f32[512,256]{1,0:T(8,128)}, f32[512,256]{1,0:T(8,128)}, f32[512,256]{1,0:T(8,128)}, f32[512,256]{1,0:T(8,128)}, /*index=5*/f32[512,256]{1,0:T(8,128)}, f32[512,256]{1,0:T(8,128)}) custom-call(s32[5]{0:T(128)} %stack.23.where_ref, f32[512,256]{1,0:T(8,128)} %refs_0_.1, f32[512,256]{1,0:T(8,128)} %refs_1_.1, ...), custom_call_target="tpu_custom_call" | custom-call | flops 1 | bytes 5242880 | tf_op jit(solution)/shard_map/pallas_call | solution.py:46
  92.3 4.7 %shard_map.100 = (f32[512,256]{1,0:T(8,128)}, bf16[3,512,1024]{2,1,0:T(8,128)(2,1)}) custom-call(s32[5]{0:T(128)} %stack.23.where_ref, bf16[512,256]{1,0:T(8,128)(2,1)} %shard_map.96.refs_8_.refs_0_, bf16[512,256]{1,0:T(8,128)(2,1)} %copy-done.8, bf16[512,256]{1,0:T(8,128)(2,1)} %copy-done.21, bf16[512,256]{1,0:T(8,128)(2,1)} %collective-permute-done.15.refs_3_, ...), custom_call_target="tpu_custom_call" | custom-call | flops 805306368 | bytes 5242880 | tf_op jit(solution)/shard_map/pallas_call | solution.py:46
  101.2 3.4 %shard_map.101 = (f32[512,256]{1,0:T(8,128)}, f32[512,256]{1,0:T(8,128)}, bf16[512,256]{1,0:T(8,128)(2,1)}) custom-call(s32[5]{0:T(128)} %stack.23.where_ref, bf16[1024,256]{1,0:T(8,128)(2,1)} %bitcast.50, bf16[512,1024]{1,0:T(8,128)(2,1)} %shard_map.98.left, f32[512,256]{1,0:T(8,128)} %get-tuple-element.29.num, f32[512,256]{1,0:T(8,128)} %get-tuple-element.30.den, ...), custom_call_target="tpu_custom_call" | custom-call | flops 268435456 | bytes 5242880 | tf_op jit(solution)/shard_map/pallas_call | solution.py:46
  104.6 5.7 %collective-permute-start.32 = (bf16[512,256]{1,0:T(8,128)(2,1)}, bf16[512,256]{1,0:T(8,128)(2,1)S(1)}, u32[]{:S(2)}, u32[]{:S(2)}) collective-permute-start(bf16[512,256]{1,0:T(8,128)(2,1)} %get-tuple-element.32.own), channel_id=1, source_target_pairs={{0,126},{1,127},{2,124},{3,125},{4,10},{5,11},{6,8},{7,9},{8,6},{9... | collective-permute-start | bytes 786440 | tf_op jit(solution)/shard_map/ppermute | solution.py:22
  110.3 2.7 %collective-permute-done.30.pair = bf16[512,256]{1,0:T(8,128)(2,1)S(1)} collective-permute-done((bf16[512,256]{1,0:T(8,128)(2,1)}, bf16[512,256]{1,0:T(8,128)(2,1)S(1)}, u32[]{:S(2)}, u32[]{:S(2)}) %collective-permute-start.30) | collective-permute-done | bytes 262176 | tf_op jit(solution)/shard_map/ppermute | solution.py:22
  113.7 2.6 %shard_map.102 = bf16[32,2,16,256]{3,2,1,0:T(8,128)(2,1)} custom-call(s32[5]{0:T(128)} %stack.23.where_ref, bf16[512,1024]{1,0:T(8,128)(2,1)} %get-tuple-element.26.right_ref, bf16[512,256]{1,0:T(8,128)(2,1)} %get-tuple-element.32.own, bf16[512,256]{1,0:T(8,128)(2,1)} %copy-done.7), custom_call_target="tpu_custom_call" | custom-call | flops 268435456 | bytes 5242880 | tf_op jit(solution)/shard_map/pallas_call | solution.py:46
  116.4 8.2 %all-to-all-start.2 = ((bf16[64,16,256]{2,1,0:T(8,128)(2,1)}), bf16[64,16,256]{2,1,0:T(8,128)(2,1)S(1)}, u32[]{:S(2)}, u32[]{:S(2)}) async-start(bf16[64,16,256]{2,1,0:T(8,128)(2,1)} %bitcast.49), calls=%async_computation.2 | async-start | bytes 1048576 | tf_op jit(solution)/shard_map/all_to_all | solution.py:241
  124.6 2.9 %collective-permute-start.31 = (bf16[512,256]{1,0:T(8,128)(2,1)S(1)}, bf16[512,256]{1,0:T(8,128)(2,1)S(1)}, u32[]{:S(2)}, u32[]{:S(2)}) collective-permute-start(bf16[512,256]{1,0:T(8,128)(2,1)S(1)} %copy-done.6), channel_id=1, source_target_pairs={{0,6},{1,7},{2,4},{3,5},{4,2},{5,3},{6,0},{7,1},{8,14},{9,15},{10,... | collective-permute-start | bytes 786440 | tf_op jit(solution)/shard_map/ppermute | solution.py:22
  128.3 3.2 %shard_map.103 = (f32[512,256]{1,0:T(8,128)}, f32[512,256]{1,0:T(8,128)}, f32[512,256]{1,0:T(8,128)}, f32[256,256]{1,0:T(8,128)}) custom-call(s32[5]{0:T(128)} %stack.23.where_ref, f32[512,256]{1,0:T(8,128)} %get-tuple-element.33.log, f32[512,256]{1,0:T(8,128)} %get-tuple-element.34.state, f32[512,256]{1,0:T(8,128)} %get-tuple-element.35.effect, ...), custom_call_target="tpu_custom_call" | custom-call | flops 1 | bytes 5242880 | tf_op jit(solution)/shard_map/pallas_call | solution.py:46
  131.4 8.6 %collective-permute-done.31.inner = bf16[512,256]{1,0:T(8,128)(2,1)S(1)} collective-permute-done((bf16[512,256]{1,0:T(8,128)(2,1)S(1)}, bf16[512,256]{1,0:T(8,128)(2,1)S(1)}, u32[]{:S(2)}, u32[]{:S(2)}) %collective-permute-start.31) | collective-permute-done | bytes 262176 | tf_op jit(solution)/shard_map/ppermute | solution.py:22
  140.7 3.7 %shard_map.104.partial = f32[512,256]{1,0:T(8,128)} custom-call(s32[5]{0:T(128)} %stack.23.where_ref, bf16[512,256]{1,0:T(8,128)(2,1)} %get-tuple-element.32.own, bf16[512,256]{1,0:T(8,128)(2,1)} %copy-done.7, bf16[512,256]{1,0:T(8,128)(2,1)} %copy-done.17, bf16[512,256]{1,0:T(8,128)(2,1)} %copy-done.16, bf16[3,512,1024]{2,1,0:T(8,128)(2,1)} %get-tuple-element.39.near_ref), custom_call_target="tpu_custom_call" | custom-call | flops 536870912 | bytes 5242880 | tf_op jit(solution)/shard_map/pallas_call | solution.py:46
  145.3 3.6 %shard_map.105.num = f32[512,256]{1,0:T(8,128)} custom-call(s32[5]{0:T(128)} %stack.23.where_ref, f32[512,256]{1,0:T(8,128)} %get-tuple-element.38.num, f32[512,256]{1,0:T(8,128)} %shard_map.104.partial, bf16[512,256]{1,0:T(8,128)(2,1)} %copy-done.22, bf16[512,256]{1,0:T(8,128)(2,1)} %copy-done.23, bf16[3,512,1024]{2,1,0:T(8,128)(2,1)} %get-tuple-element.39.near_ref), custom_call_target="tpu_custom_call" | custom-call | flops 268435456 | bytes 5242880 | tf_op jit(solution)/shard_map/pallas_call | solution.py:46
  149.7 3.3 %shard_map.106 = (f32[512,256]{1,0:T(8,128)}, f32[256,256]{1,0:T(8,128)}) custom-call(s32[5]{0:T(128)} %stack.23.where_ref, bf16[1024,256]{1,0:T(8,128)(2,1)} %bitcast.51, bf16[512,1024]{1,0:T(8,128)(2,1)} %shard_map.98.left, f32[512,256]{1,0:T(8,128)} %shard_map.105.num, f32[512,256]{1,0:T(8,128)} %get-tuple-element.40.den, ...), custom_call_target="tpu_custom_call" | custom-call | flops 268435456 | bytes 5242880 | tf_op jit(solution)/shard_map/pallas_call | solution.py:46
  (160 shorter events, 47.1 us)
Async XLA Ops:
  1.7 22.6 %collective-permute-start.26 = (f32[256,256]{1,0:T(8,128)S(1)}, f32[256,256]{1,0:T(8,128)S(1)}, u32[]{:S(2)}, u32[]{:S(2)}) collective-permute-start(f32[256,256]{1,0:T(8,128)S(1)} %constant_dynamic-slice_fusion.3), channel_id=1, source_target_pairs={{0,1},{1,0},{2,3},{3,2},{4,5},{5,4},{6,7},{7,6},{8,9},{9,8},{10,11... | collective-permute-start | bytes 786440 | tf_op jit(solution)/shard_map/ppermute | solution.py:22
  2.9 23.6 %collective-permute-start.27 = (f32[256,256]{1,0:T(8,128)S(1)}, f32[256,256]{1,0:T(8,128)}, u32[]{:S(2)}, u32[]{:S(2)}) collective-permute-start(f32[256,256]{1,0:T(8,128)S(1)} %constant_dynamic-slice_fusion.2), channel_id=1, source_target_pairs={{0,1},{1,0},{2,3},{3,2},{4,5},{5,4},{6,7},{7,6},{8,9},{9,8},{10,11... | collective-permute-start | bytes 786440 | tf_op jit(solution)/shard_map/ppermute | solution.py:22
  15.7 14.0 %collective-permute-start.28 = (f32[256,256]{1,0:T(8,128)}, f32[256,256]{1,0:T(8,128)S(1)}, u32[]{:S(2)}, u32[]{:S(2)}) collective-permute-start(f32[256,256]{1,0:T(8,128)} %constant_dynamic-slice_fusion.1), channel_id=1, source_target_pairs={{0,1},{1,0},{2,3},{3,2},{4,5},{5,4},{6,7},{7,6},{8,9},{9,8},{10,11... | collective-permute-start | bytes 786440 | tf_op jit(solution)/shard_map/ppermute | solution.py:22
  17.4 13.9 %collective-permute-start.29 = (f32[256,256]{1,0:T(8,128)}, f32[256,256]{1,0:T(8,128)S(1)}, u32[]{:S(2)}, u32[]{:S(2)}) collective-permute-start(f32[256,256]{1,0:T(8,128)} %constant_dynamic-slice_fusion), channel_id=1, source_target_pairs={{0,1},{1,0},{2,3},{3,2},{4,5},{5,4},{6,7},{7,6},{8,9},{9,8},{10,11... | collective-permute-start | bytes 786440 | tf_op jit(solution)/shard_map/ppermute | solution.py:22
  21.5 15.1 %collective-permute-start.6 = (bf16[4,16,1024]{2,1,0:T(8,128)(2,1)}, bf16[4,16,1024]{2,1,0:T(8,128)(2,1)S(1)}, u32[]{:S(2)}, u32[]{:S(2)}) collective-permute-start(bf16[4,16,1024]{2,1,0:T(8,128)(2,1)} %get-tuple-element.50), channel_id=1, source_target_pairs={{0,48},{1,56},{2,50},{3,58},{4,52},{5,60},{6,54},{7,62},{8,112},{9... | collective-permute-start | bytes 393224 | tf_op jit(solution)/shard_map/ppermute | solution.py:22
  24.3 13.8 %collective-permute-start.3 = (bf16[4,16,1024]{2,1,0:T(8,128)(2,1)}, bf16[4,16,1024]{2,1,0:T(8,128)(2,1)}, u32[]{:S(2)}, u32[]{:S(2)}) collective-permute-start(bf16[4,16,1024]{2,1,0:T(8,128)(2,1)} %get-tuple-element.53), channel_id=1, source_target_pairs={{0,0},{1,8},{2,2},{3,10},{4,4},{5,12},{6,6},{7,14},{8,64},{9,72},{... | collective-permute-start | bytes 393224 | tf_op jit(solution)/shard_map/ppermute | solution.py:22
  29.7 36.9 %collective-permute-start.18 = (bf16[3,64,1024]{2,1,0:T(8,128)(2,1)}, bf16[3,64,1024]{2,1,0:T(8,128)(2,1)S(1)}, u32[]{:S(2)}, u32[]{:S(2)}) collective-permute-start(bf16[3,64,1024]{2,1,0:T(8,128)(2,1)} %get-tuple-element.48), channel_id=1, source_target_pairs={{0,0},{1,4},{2,8},{3,12},{4,1},{5,5},{6,9},{7,13},{8,2},{9,6},{10,... | collective-permute-start | bytes 1179656 | tf_op jit(solution)/shard_map/ppermute | solution.py:22
  31.3 17.0 %collective-permute-start.12 = (bf16[512,256]{1,0:T(8,128)(2,1)}, bf16[512,256]{1,0:T(8,128)(2,1)S(1)}, u32[]{:S(2)}, u32[]{:S(2)}) collective-permute-start(bf16[512,256]{1,0:T(8,128)(2,1)} %shard_map.96.refs_8_.refs_0_), channel_id=1, source_target_pairs={{0,2},{1,3},{2,0},{3,1},{4,6},{5,7},{6,4},{7,5},{8,10},{9,11},{10,... | collective-permute-start | bytes 786440 | tf_op jit(solution)/shard_map/ppermute | solution.py:22
  36.6 15.0 %collective-permute-start.15 = (bf16[512,256]{1,0:T(8,128)(2,1)}, bf16[512,256]{1,0:T(8,128)(2,1)}, u32[]{:S(2)}, u32[]{:S(2)}) collective-permute-start(bf16[512,256]{1,0:T(8,128)(2,1)} %shard_map.96.refs_8_.refs_0_), channel_id=1, source_target_pairs={{0,126},{1,127},{2,124},{3,125},{4,10},{5,11},{6,8},{7,9},{8,6},{9... | collective-permute-start | bytes 786440 | tf_op jit(solution)/shard_map/ppermute | solution.py:22
  38.1 23.2 %collective-permute-start.14 = (bf16[512,256]{1,0:T(8,128)(2,1)}, bf16[512,256]{1,0:T(8,128)(2,1)S(1)}, u32[]{:S(2)}, u32[]{:S(2)}) collective-permute-start(bf16[512,256]{1,0:T(8,128)(2,1)} %shard_map.96.refs_8_.refs_0_), channel_id=1, source_target_pairs={{0,6},{1,7},{2,4},{3,5},{4,2},{5,3},{6,0},{7,1},{8,14},{9,15},{10,... | collective-permute-start | bytes 786440 | tf_op jit(solution)/shard_map/ppermute | solution.py:22
  41.0 29.4 %all-to-all-start.1 = ((bf16[16,64,256]{2,1,0:T(8,128)(2,1)}), bf16[16,64,256]{2,1,0:T(8,128)(2,1)S(1)}, u32[]{:S(2)}, u32[]{:S(2)}) async-start(bf16[16,64,256]{2,1,0:T(8,128)(2,1)} %bitcast.17), calls=%async_computation.1 | async-start | bytes 1048576 | tf_op jit(solution)/shard_map/all_to_all | solution.py:219
  48.4 14.0 %collective-permute-start.7 = (bf16[64,1024]{1,0:T(8,128)(2,1)}, bf16[64,1024]{1,0:T(8,128)(2,1)S(1)}, u32[]{:S(2)}, u32[]{:S(2)}) collective-permute-start(bf16[64,1024]{1,0:T(8,128)(2,1)} %bitcast.10.refs_0_), channel_id=1, source_target_pairs={{0,1},{1,0},{2,3},{3,2},{4,5},{5,4},{6,7},{7,6},{8,9},{9,8},{10,11... | collective-permute-start | bytes 393224 | tf_op jit(solution)/shard_map/ppermute | solution.py:22
  61.3 22.4 %collective-permute-start.20 = (bf16[3,64,1024]{2,1,0:T(8,128)(2,1)S(1)}, bf16[3,64,1024]{2,1,0:T(8,128)(2,1)}, u32[]{:S(2)}, u32[]{:S(2)}) collective-permute-start(bf16[3,64,1024]{2,1,0:T(8,128)(2,1)S(1)} %get-tuple-element.49), channel_id=1, source_target_pairs={{0,8},{1,12},{2,0},{3,4},{4,9},{5,13},{6,1},{7,5},{8,10},{9,14},{1... | collective-permute-start | bytes 1179656 | tf_op jit(solution)/shard_map/ppermute | solution.py:22
  62.4 21.4 %collective-permute-start.21 = (bf16[3,64,1024]{2,1,0:T(8,128)(2,1)S(1)}, bf16[3,64,1024]{2,1,0:T(8,128)(2,1)}, u32[]{:S(2)}, u32[]{:S(2)}) collective-permute-start(bf16[3,64,1024]{2,1,0:T(8,128)(2,1)S(1)} %get-tuple-element.46), channel_id=1, source_target_pairs={{0,12},{1,8},{2,4},{3,0},{4,13},{5,9},{6,5},{7,1},{8,14},{9,10},{1... | collective-permute-start | bytes 1179656 | tf_op jit(solution)/shard_map/ppermute | solution.py:22
  64.0 20.3 %collective-permute-start.16 = (bf16[512,256]{1,0:T(8,128)(2,1)S(1)}, bf16[512,256]{1,0:T(8,128)(2,1)}, u32[]{:S(2)}, u32[]{:S(2)}) collective-permute-start(bf16[512,256]{1,0:T(8,128)(2,1)S(1)} %collective-permute-done.12.refs_9_.refs_1_), channel_id=1, source_target_pairs={{0,6},{1,7},{2,4},{3,5},{4,2},{5,3},{6,0},{7,1},{8,14},{9,15},{10,... | collective-permute-start | bytes 786440 | tf_op jit(solution)/shard_map/ppermute | solution.py:22
  66.6 20.1 %collective-permute-start.17 = (bf16[512,256]{1,0:T(8,128)(2,1)}, bf16[512,256]{1,0:T(8,128)(2,1)}, u32[]{:S(2)}, u32[]{:S(2)}) collective-permute-start(bf16[512,256]{1,0:T(8,128)(2,1)} %collective-permute-done.15.refs_3_), channel_id=1, source_target_pairs={{0,2},{1,3},{2,0},{3,1},{4,6},{5,7},{6,4},{7,5},{8,10},{9,11},{10,... | collective-permute-start | bytes 786440 | tf_op jit(solution)/shard_map/ppermute | solution.py:22
  70.5 26.6 %collective-permute-start.13 = (bf16[1024,256]{1,0:T(8,128)(2,1)S(1)}, bf16[1024,256]{1,0:T(8,128)(2,1)S(1)}, u32[]{:S(2)}, u32[]{:S(2)}) collective-permute-start(bf16[1024,256]{1,0:T(8,128)(2,1)S(1)} %bitcast.47), channel_id=1, source_target_pairs={{0,1},{1,0},{2,3},{3,2},{4,5},{5,4},{6,7},{7,6},{8,9},{9,8},{10,11... | collective-permute-start | bytes 1572872 | tf_op jit(solution)/shard_map/ppermute | solution.py:22
  78.2 22.1 %all-to-all-start = ((bf16[64,16,256]{2,1,0:T(8,128)(2,1)}), bf16[64,16,256]{2,1,0:T(8,128)(2,1)S(1)}, u32[]{:S(2)}, u32[]{:S(2)}) async-start(bf16[64,16,256]{2,1,0:T(8,128)(2,1)} %bitcast.52), calls=%async_computation | async-start | bytes 1048576 | tf_op jit(solution)/shard_map/all_to_all | solution.py:241
  104.6 23.3 %collective-permute-start.32 = (bf16[512,256]{1,0:T(8,128)(2,1)}, bf16[512,256]{1,0:T(8,128)(2,1)S(1)}, u32[]{:S(2)}, u32[]{:S(2)}) collective-permute-start(bf16[512,256]{1,0:T(8,128)(2,1)} %get-tuple-element.32.own), channel_id=1, source_target_pairs={{0,126},{1,127},{2,124},{3,125},{4,10},{5,11},{6,8},{7,9},{8,6},{9... | collective-permute-start | bytes 786440 | tf_op jit(solution)/shard_map/ppermute | solution.py:22
  116.4 32.5 %all-to-all-start.2 = ((bf16[64,16,256]{2,1,0:T(8,128)(2,1)}), bf16[64,16,256]{2,1,0:T(8,128)(2,1)S(1)}, u32[]{:S(2)}, u32[]{:S(2)}) async-start(bf16[64,16,256]{2,1,0:T(8,128)(2,1)} %bitcast.49), calls=%async_computation.2 | async-start | bytes 1048576 | tf_op jit(solution)/shard_map/all_to_all | solution.py:241
  124.6 15.5 %collective-permute-start.31 = (bf16[512,256]{1,0:T(8,128)(2,1)S(1)}, bf16[512,256]{1,0:T(8,128)(2,1)S(1)}, u32[]{:S(2)}, u32[]{:S(2)}) collective-permute-start(bf16[512,256]{1,0:T(8,128)(2,1)S(1)} %copy-done.6), channel_id=1, source_target_pairs={{0,6},{1,7},{2,4},{3,5},{4,2},{5,3},{6,0},{7,1},{8,14},{9,15},{10,... | collective-permute-start | bytes 786440 | tf_op jit(solution)/shard_map/ppermute | solution.py:22
  127.4 17.0 %collective-permute-start.33 = (bf16[512,256]{1,0:T(8,128)(2,1)}, bf16[512,256]{1,0:T(8,128)(2,1)S(1)}, u32[]{:S(2)}, u32[]{:S(2)}) collective-permute-start(bf16[512,256]{1,0:T(8,128)(2,1)} %copy-done.7), channel_id=1, source_target_pairs={{0,6},{1,7},{2,4},{3,5},{4,2},{5,3},{6,0},{7,1},{8,14},{9,15},{10,... | collective-permute-start | bytes 786440 | tf_op jit(solution)/shard_map/ppermute | solution.py:22
  127.9 16.6 %collective-permute-start.34 = (bf16[512,256]{1,0:T(8,128)(2,1)S(1)}, bf16[512,256]{1,0:T(8,128)(2,1)S(1)}, u32[]{:S(2)}, u32[]{:S(2)}) collective-permute-start(bf16[512,256]{1,0:T(8,128)(2,1)S(1)} %collective-permute-done.32.outer), channel_id=1, source_target_pairs={{0,2},{1,3},{2,0},{3,1},{4,6},{5,7},{6,4},{7,5},{8,10},{9,11},{10,... | collective-permute-start | bytes 786440 | tf_op jit(solution)/shard_map/ppermute | solution.py:22
  131.4 21.6 %collective-permute-start.36 = (f32[256,256]{1,0:T(8,128)}, f32[256,256]{1,0:T(8,128)S(1)}, u32[]{:S(2)}, u32[]{:S(2)}) collective-permute-start(f32[256,256]{1,0:T(8,128)} %get-tuple-element.45), channel_id=1, source_target_pairs={{0,1},{1,0},{2,3},{3,2},{4,5},{5,4},{6,7},{7,6},{8,9},{9,8},{10,11... | collective-permute-start | bytes 786440 | tf_op jit(solution)/shard_map/ppermute | solution.py:22
  (50 other events, 442.5 us)

commit v2 on v1

--- a/solution.py
+++ b/solution.py
@@ -42,13 +42,17 @@
 VECTORS = pl.BlockSpec(memory_space=pltpu.VMEM)
 
 
-def call(kernel, outs, where, operands, flops, scratch=()):
+SMALL = ("coeff", "near", "near_outer", "raise", "join")
+
+
+def call(kernel, outs, where, operands, name, flops, scratch=()):
     return pl.pallas_call(
         kernel,
         out_shape=outs,
         in_specs=[SCALARS] + [VECTORS] * len(operands),
         out_specs=[VECTORS] * len(outs),
         scratch_shapes=scratch,
+        compiler_params=pltpu.CompilerParams(vmem_limit_bytes=20 << 20) if name in SMALL else None,
         cost_estimate=pl.CostEstimate(flops=flops, bytes_accessed=5 << 20, transcendentals=0),
     )(where, *operands)
 
@@ -128,7 +132,7 @@
     for half in range(2):
         rows = slice(half * 256, half * 256 + 256)
         log, state, effect, load = (
-            (received[i][...] if half else whole[i][mine, :]).T for i in range(4)
+            (received[i] if half else whole[i])[mine, :].T for i in range(4)
         )
         velocity = jnp.exp(log)
         state_rate = jnp.exp(-state) - velocity
@@ -226,10 +230,10 @@
     parts = [move(pick(dense_near, quarter ^ s), functools.partial(near_target, s=s)) for s in range(4)]
     parts = parts + [move(parts[s], partner) for s in range(4)]
 
-    own, theirs = call(raise_kernel, [HALF, HALF], where, (slip_log,), 1)
-    (slip,) = call(join_kernel, [SLIP], where, (own, move(theirs, partner)), 1)
+    own, theirs = call(raise_kernel, [HALF, HALF], where, (slip_log,), "raise", 1)
+    (slip,) = call(join_kernel, [SLIP], where, (own, move(theirs, partner)), "join", 1)
     arrays = (slip_log, fault_state, direct_effect, loading)
-    received = [move(lax.dynamic_slice_in_dim(v, (1 - core) * 256, 256, 0), partner) for v in arrays]
+    received = [move(v, partner) for v in arrays]
 
     def exchange(slip):
         pair = move(slip, zl)
@@ -244,26 +248,30 @@
         return lax.dynamic_update_slice(own, move(other, partner), ((1 - core) * 256, 0))
 
     pieces, crossed = exchange(slip)
-    sent, right = call(coeff_first_kernel, [SENT, RIGHT], where, (*right_parts, *pieces[:2]), 1 << 28)
+    sent, right = call(coeff_first_kernel, [SENT, RIGHT], where, (*right_parts, *pieces[:2]), "coeff_first", 1 << 28)
     coeff = all_to_all(sent)
-    (left,) = call(left_kernel, [LEFT], where, lefts, 1 << 20)
+    (left,) = call(left_kernel, [LEFT], where, lefts, "left", 1 << 20)
     log, effect, load, num, den, mid_state, sum_state = call(
-        prepare_first_kernel, [STATE] * 7, where, (*arrays, *received), 1
-    )
-    num, near = call(near_first_kernel, [STATE, NEAR], where, (*pieces, *crossed, *parts, num), 3 << 28)
-    mid_log, sum_log, slip = call(far_first_kernel, [STATE, STATE, SLIP], where, (coeff, left, num, den, log), 1 << 28)
+        prepare_first_kernel, [STATE] * 7, where, (*arrays, *received), "prepare_first", 1
+    )
+    num, near = call(near_first_kernel, [STATE, NEAR], where, (*pieces, *crossed, *parts, num), "near_first", 3 << 28)
+    mid_log, sum_log, slip = call(
+        far_first_kernel, [STATE, STATE, SLIP], where, (coeff, left, num, den, log), "far_first", 1 << 28
+    )
 
     pieces, crossed = exchange(slip)
-    (sent,) = call(coeff_kernel, [SENT], where, (right, *pieces[:2]), 1 << 28)
+    (sent,) = call(coeff_kernel, [SENT], where, (right, *pieces[:2]), "coeff", 1 << 28)
     coeff = all_to_all(sent)
-    (partial,) = call(near_kernel, [STATE], where, (*pieces, near), 2 << 28)
+    (partial,) = call(near_kernel, [STATE], where, (*pieces, near), "near", 2 << 28)
     num, den, own, other = call(
         prepare_second_kernel, [STATE, STATE, STATE, TURNED], where,
-        (mid_log, mid_state, effect, load, sum_state), 1,
-    )
-    (num,) = call(near_outer_kernel, [STATE], where, (num, partial, *crossed, near), 1 << 28)
+        (mid_log, mid_state, effect, load, sum_state), "prepare_second", 1,
+    )
+    (num,) = call(near_outer_kernel, [STATE], where, (num, partial, *crossed, near), "near_outer", 1 << 28)
     new_state = restored(own, other)
-    own, other = call(far_second_kernel, [STATE, TURNED], where, (coeff, left, num, den, sum_log), 1 << 28)
+    own, other = call(
+        far_second_kernel, [STATE, TURNED], where, (coeff, left, num, den, sum_log), "far_second", 1 << 28
+    )
     return restored(own, other), new_state
 
 

time: 157 us -> 161 us (1.025)
  Pallas kernels: 37.7 us -> 30.1 us
  waiting for transfers between devices: 36.4 us -> 43.9 us
  starting transfers between devices: 62.7 us -> 66.7 us
    pallas_call x12, Pallas kernels: 37.7 us -> 30.1 us  [call(): pl.pallas_call(kernel, out_shape=outs, in_specs=[SCALARS] + [VECTORS] * l...]
    ppermute x37, waiting for transfers between devices: 36.4 us -> 42.7 us  [move(): return lax.ppermute(value, ALL, [(d, target(d)) for d in range(COUNT)])]
    all_to_all x2, starting transfers between devices: 13.6 us -> 19 us  [all_to_all(): lax.all_to_all(sent.reshape(64, 16, 256), ('row', 'chip'), 0, 0)]
    dynamic_slice x4 -> x0, local copies, waits for them, and re-layouts: 3.53 us -> none  [on_device(): lax.dynamic_slice_in_dim(v, (1 - core) * 256, 256, 0)]
    unnamed x69 -> x75, local copies, waits for them, and re-layouts: 5.63 us -> 8 us
  transfers between devices with their start and end apart: 40 -> 40, of which waited for: 10 -> 11; matrix products, arithmetic and copies ran while one was open for 7% -> 5% of each run, Pallas kernels for 22% -> 16%
where the time goes in v2:
time: 161 us; the launch traced here: 159 us
  starting transfers between devices  66.7 us (41%)
  waiting for transfers between devices  43.9 us (27%)
  Pallas kernels  30.1 us (19%)
  local copies, waits for them, and re-layouts  14.6 us (9%)
  other arithmetic  2.34 us (1%)
    ppermute x37, waiting for transfers between devices, move(): return lax.ppermute(value, ALL, [(d, target(d)) for d in range(COUNT)])  42.7 us
    ppermute x37, starting transfers between devices, move(): return lax.ppermute(value, ALL, [(d, target(d)) for d in range(COUNT)])  42.2 us
    pallas_call x12, Pallas kernels, call(): pl.pallas_call(kernel, out_shape=outs, in_specs=[SCALARS] + [VECTORS] * l...  30.1 us
    all_to_all x2, starting transfers between devices, all_to_all(): lax.all_to_all(sent.reshape(64, 16, 256), ('row', 'chip'), 0, 0)  19 us
    unnamed x75, local copies, waits for them, and re-layouts  8 us
    all_to_all x1, starting transfers between devices, on_device(): left = lax.all_to_all(left_out, ('chip', 'core'), 0, 0).reshape(1024, 256)  5.54 us
  transfers between devices with their start and end apart: 40, of which 11 were waited for; matrix products, arithmetic and copies ran while one was open for 5% of the time, Pallas kernels for 16%

profile of v2, /device:TPU:0, one launch (start us, length us, event | category | flops | bytes accessed | tf_op | source)
XLA Modules:
  0.0 158.8 jit_solution(5189337341582953601)
XLA Ops:
  3.6 2.1 %collective-permute-start = (bf16[4,16,1024]{2,1,0:T(8,128)(2,1)S(1)}, bf16[4,16,1024]{2,1,0:T(8,128)(2,1)S(1)}, u32[]{:S(2)}, u32[]{:S(2)}) collective-permute-start(bf16[4,16,1024]{2,1,0:T(8,128)(2,1)S(1)} %get-tuple-element.56), channel_id=1, source_target_pairs={{0,2},{1,3},{2,0},{3,1},{4,6},{5,7},{6,4},{7,5},{8,10},{9,11},{10,... | collective-permute-start | bytes 393224 | tf_op jit(solution)/shard_map/ppermute | solution.py:22
  5.7 3.6 %collective-permute-start.1 = (bf16[4,16,1024]{2,1,0:T(8,128)(2,1)S(1)}, bf16[4,16,1024]{2,1,0:T(8,128)(2,1)S(1)}, u32[]{:S(2)}, u32[]{:S(2)}) collective-permute-start(bf16[4,16,1024]{2,1,0:T(8,128)(2,1)S(1)} %get-tuple-element.55), channel_id=1, source_target_pairs={{0,4},{1,5},{2,6},{3,7},{4,0},{5,1},{6,2},{7,3},{8,12},{9,13},{10,... | collective-permute-start | bytes 393224 | tf_op jit(solution)/shard_map/ppermute | solution.py:22
  10.1 6.4 %collective-permute-done.1 = bf16[4,16,1024]{2,1,0:T(8,128)(2,1)S(1)} collective-permute-done((bf16[4,16,1024]{2,1,0:T(8,128)(2,1)S(1)}, bf16[4,16,1024]{2,1,0:T(8,128)(2,1)S(1)}, u32[]{:S(2)}, u32[]{:S(2)}) %collective-permute-start.1) | collective-permute-done | bytes 131104 | tf_op jit(solution)/shard_map/ppermute | solution.py:22
  16.5 1.9 %collective-permute-done.2 = bf16[4,16,1024]{2,1,0:T(8,128)(2,1)S(1)} collective-permute-done((bf16[4,16,1024]{2,1,0:T(8,128)(2,1)S(1)}, bf16[4,16,1024]{2,1,0:T(8,128)(2,1)S(1)}, u32[]{:S(2)}, u32[]{:S(2)}) %collective-permute-start.2) | collective-permute-done | bytes 131104 | tf_op jit(solution)/shard_map/ppermute | solution.py:22
  20.2 2.8 %collective-permute-start.6 = (bf16[4,16,1024]{2,1,0:T(8,128)(2,1)}, bf16[4,16,1024]{2,1,0:T(8,128)(2,1)}, u32[]{:S(2)}, u32[]{:S(2)}) collective-permute-start(bf16[4,16,1024]{2,1,0:T(8,128)(2,1)} %get-tuple-element.50), channel_id=1, source_target_pairs={{0,48},{1,56},{2,50},{3,58},{4,52},{5,60},{6,54},{7,62},{8,112},{9... | collective-permute-start | bytes 393224 | tf_op jit(solution)/shard_map/ppermute | solution.py:22
  23.0 2.3 %collective-permute-start.3 = (bf16[4,16,1024]{2,1,0:T(8,128)(2,1)}, bf16[4,16,1024]{2,1,0:T(8,128)(2,1)}, u32[]{:S(2)}, u32[]{:S(2)}) collective-permute-start(bf16[4,16,1024]{2,1,0:T(8,128)(2,1)} %get-tuple-element.53), channel_id=1, source_target_pairs={{0,0},{1,8},{2,2},{3,10},{4,4},{5,12},{6,6},{7,14},{8,64},{9,72},{... | collective-permute-start | bytes 393224 | tf_op jit(solution)/shard_map/ppermute | solution.py:22
  28.3 6.2 %collective-permute-start.15 = (bf16[512,256]{1,0:T(8,128)(2,1)S(1)}, bf16[512,256]{1,0:T(8,128)(2,1)S(1)}, u32[]{:S(2)}, u32[]{:S(2)}) collective-permute-start(bf16[512,256]{1,0:T(8,128)(2,1)S(1)} %shard_map.96.refs_8_.refs_0_), channel_id=1, source_target_pairs={{0,126},{1,127},{2,124},{3,125},{4,10},{5,11},{6,8},{7,9},{8,6},{9... | collective-permute-start | bytes 786440 | tf_op jit(solution)/shard_map/ppermute | solution.py:22
  37.1 2.4 %collective-permute-start.10 = (bf16[64,1024]{1,0:T(8,128)(2,1)}, bf16[64,1024]{1,0:T(8,128)(2,1)S(1)}, u32[]{:S(2)}, u32[]{:S(2)}) collective-permute-start(bf16[64,1024]{1,0:T(8,128)(2,1)} %bitcast.13.refs_3_), channel_id=1, source_target_pairs={{0,1},{1,0},{2,3},{3,2},{4,5},{5,4},{6,7},{7,6},{8,9},{9,8},{10,11... | collective-permute-start | bytes 393224 | tf_op jit(solution)/shard_map/ppermute | solution.py:22
  43.8 8.4 %collective-permute-done.14.refs_2_ = bf16[512,256]{1,0:T(8,128)(2,1)S(1)} collective-permute-done((bf16[512,256]{1,0:T(8,128)(2,1)S(1)}, bf16[512,256]{1,0:T(8,128)(2,1)S(1)}, u32[]{:S(2)}, u32[]{:S(2)}) %collective-permute-start.14) | collective-permute-done | bytes 262176 | tf_op jit(solution)/shard_map/ppermute | solution.py:22
  58.4 5.5 %all-to-all-start.1 = ((bf16[16,64,256]{2,1,0:T(8,128)(2,1)}), bf16[16,64,256]{2,1,0:T(8,128)(2,1)S(1)}, u32[]{:S(2)}, u32[]{:S(2)}) async-start(bf16[16,64,256]{2,1,0:T(8,128)(2,1)} %bitcast.17), calls=%async_computation.1 | async-start | bytes 1048576 | tf_op jit(solution)/shard_map/all_to_all | solution.py:223
  64.5 7.5 %collective-permute-done.20.refs_8_ = bf16[3,64,1024]{2,1,0:T(8,128)(2,1)} collective-permute-done((bf16[3,64,1024]{2,1,0:T(8,128)(2,1)}, bf16[3,64,1024]{2,1,0:T(8,128)(2,1)}, u32[]{:S(2)}, u32[]{:S(2)}) %collective-permute-start.20) | collective-permute-done | bytes 393248 | tf_op jit(solution)/shard_map/ppermute | solution.py:22
  72.0 5.1 %collective-permute-done.21.refs_9_ = bf16[3,64,1024]{2,1,0:T(8,128)(2,1)} collective-permute-done((bf16[3,64,1024]{2,1,0:T(8,128)(2,1)S(1)}, bf16[3,64,1024]{2,1,0:T(8,128)(2,1)}, u32[]{:S(2)}, u32[]{:S(2)}) %collective-permute-start.21) | collective-permute-done | bytes 393248 | tf_op jit(solution)/shard_map/ppermute | solution.py:22
  78.4 3.0 %shard_map.97 = (bf16[32,2,16,256]{3,2,1,0:T(8,128)(2,1)}, bf16[512,1024]{1,0:T(8,128)(2,1)}) custom-call(s32[5]{0:T(128)} %copy-done.12, bf16[64,1024]{1,0:T(8,128)(2,1)} %bitcast.10.refs_0_, bf16[64,1024]{1,0:T(8,128)(2,1)} %bitcast.55, bf16[64,1024]{1,0:T(8,128)(2,1)} %bitcast.12.refs_2_, bf16[64,1024]{1,0:T(8,128)(2,1)} %bitcast.13.refs_3_, ...), custom_call_target="tpu_custom_call" | custom-call | flops 268435456 | bytes 5242880 | tf_op jit(solution)/shard_map/pallas_call | solution.py:49
  81.4 8.0 %all-to-all-start = ((bf16[64,16,256]{2,1,0:T(8,128)(2,1)}), bf16[64,16,256]{2,1,0:T(8,128)(2,1)S(1)}, u32[]{:S(2)}, u32[]{:S(2)}) async-start(bf16[64,16,256]{2,1,0:T(8,128)(2,1)} %bitcast.51), calls=%async_computation | async-start | bytes 1048576 | tf_op jit(solution)/shard_map/all_to_all | solution.py:245
  90.6 4.4 %shard_map.99 = (f32[512,256]{1,0:T(8,128)}, f32[512,256]{1,0:T(8,128)}, f32[512,256]{1,0:T(8,128)}, f32[512,256]{1,0:T(8,128)}, f32[512,256]{1,0:T(8,128)}, /*index=5*/f32[512,256]{1,0:T(8,128)}, f32[512,256]{1,0:T(8,128)}) custom-call(s32[5]{0:T(128)} %copy-done.12, f32[512,256]{1,0:T(8,128)} %refs_0_.1, f32[512,256]{1,0:T(8,128)} %refs_1_.1, ...), custom_call_target="tpu_custom_call" | custom-call | flops 1 | bytes 5242880 | tf_op jit(solution)/shard_map/pallas_call | solution.py:49
  95.9 4.8 %shard_map.100 = (f32[512,256]{1,0:T(8,128)}, bf16[3,512,1024]{2,1,0:T(8,128)(2,1)}) custom-call(s32[5]{0:T(128)} %copy-done.12, bf16[512,256]{1,0:T(8,128)(2,1)} %copy-done.1, bf16[512,256]{1,0:T(8,128)(2,1)} %copy-done.18, bf16[512,256]{1,0:T(8,128)(2,1)} %copy-done.28, bf16[512,256]{1,0:T(8,128)(2,1)} %copy-done.27, bf16[512,256]{1,0:T(8,128)(2,1)} %copy-done.29, ...), custom_call_target="tpu_custom_call" | custom-call | flops 805306368 | bytes 5242880 | tf_op jit(solution)/shard_map/pallas_call | solution.py:49
  101.4 2.5 %shard_map.98.left = bf16[512,1024]{1,0:T(8,128)(2,1)} custom-call(s32[5]{0:T(128)} %copy-done.12, bf16[1024,256]{1,0:T(8,128)(2,1)} %bitcast.49, bf16[1024,256]{1,0:T(8,128)(2,1)} %copy-done.22), custom_call_target="tpu_custom_call" | custom-call | flops 1048576 | bytes 5242880 | tf_op jit(solution)/shard_map/pallas_call | solution.py:49
  104.8 3.5 %shard_map.101 = (f32[512,256]{1,0:T(8,128)}, f32[512,256]{1,0:T(8,128)}, bf16[512,256]{1,0:T(8,128)(2,1)}) custom-call(s32[5]{0:T(128)} %copy-done.12, bf16[1024,256]{1,0:T(8,128)(2,1)} %bitcast.50, bf16[512,1024]{1,0:T(8,128)(2,1)} %shard_map.98.left, f32[512,256]{1,0:T(8,128)} %get-tuple-element.29.num, f32[512,256]{1,0:T(8,128)} %get-tuple-element.30.den, ...), custom_call_target="tpu_custom_call" | custom-call | flops 268435456 | bytes 5242880 | tf_op jit(solution)/shard_map/pallas_call | solution.py:49
  109.9 6.6 %collective-permute-start.32 = (bf16[512,256]{1,0:T(8,128)(2,1)}, bf16[512,256]{1,0:T(8,128)(2,1)}, u32[]{:S(2)}, u32[]{:S(2)}) collective-permute-start(bf16[512,256]{1,0:T(8,128)(2,1)} %get-tuple-element.32.own), channel_id=1, source_target_pairs={{0,126},{1,127},{2,124},{3,125},{4,10},{5,11},{6,8},{7,9},{8,6},{9... | collective-permute-start | bytes 786440 | tf_op jit(solution)/shard_map/ppermute | solution.py:22
  119.8 10.9 %all-to-all-start.2 = ((bf16[64,16,256]{2,1,0:T(8,128)(2,1)}), bf16[64,16,256]{2,1,0:T(8,128)(2,1)}, u32[]{:S(2)}, u32[]{:S(2)}) async-start(bf16[64,16,256]{2,1,0:T(8,128)(2,1)} %bitcast.47), calls=%async_computation.2 | async-start | bytes 1048576 | tf_op jit(solution)/shard_map/all_to_all | solution.py:245
  130.8 2.8 %collective-permute-start.31 = (bf16[512,256]{1,0:T(8,128)(2,1)S(1)}, bf16[512,256]{1,0:T(8,128)(2,1)}, u32[]{:S(2)}, u32[]{:S(2)}) collective-permute-start(bf16[512,256]{1,0:T(8,128)(2,1)S(1)} %copy-done.7), channel_id=1, source_target_pairs={{0,6},{1,7},{2,4},{3,5},{4,2},{5,3},{6,0},{7,1},{8,14},{9,15},{10,... | collective-permute-start | bytes 786440 | tf_op jit(solution)/shard_map/ppermute | solution.py:22
  134.4 3.1 %shard_map.103 = (f32[512,256]{1,0:T(8,128)}, f32[512,256]{1,0:T(8,128)}, f32[512,256]{1,0:T(8,128)}, f32[256,256]{1,0:T(8,128)}) custom-call(s32[5]{0:T(128)} %copy-done.12, f32[512,256]{1,0:T(8,128)} %get-tuple-element.33.log, f32[512,256]{1,0:T(8,128)} %get-tuple-element.34.state, f32[512,256]{1,0:T(8,128)} %get-tuple-element.35.effect, ...), custom_call_target="tpu_custom_call" | custom-call | flops 1 | bytes 5242880 | tf_op jit(solution)/shard_map/pallas_call | solution.py:49
  137.5 8.8 %collective-permute-done.31.inner = bf16[512,256]{1,0:T(8,128)(2,1)} collective-permute-done((bf16[512,256]{1,0:T(8,128)(2,1)S(1)}, bf16[512,256]{1,0:T(8,128)(2,1)}, u32[]{:S(2)}, u32[]{:S(2)}) %collective-permute-start.31) | collective-permute-done | bytes 262176 | tf_op jit(solution)/shard_map/ppermute | solution.py:22
  153.0 3.3 %shard_map.106 = (f32[512,256]{1,0:T(8,128)}, f32[256,256]{1,0:T(8,128)}) custom-call(s32[5]{0:T(128)} %copy-done.12, bf16[1024,256]{1,0:T(8,128)(2,1)} %bitcast.24.coeff, bf16[512,1024]{1,0:T(8,128)(2,1)} %shard_map.98.left, f32[512,256]{1,0:T(8,128)} %copy-done.5, f32[512,256]{1,0:T(8,128)} %get-tuple-element.40.den, f32[512,256]{1,0:T(8,128)} %get-tuple-element.41.sum_log), custom_call_target="tpu_custom_call" | custom-call | flops 268435456 | bytes 5242880 | tf_op jit(solution)/shard_map/pallas_call | solution.py:49
  (162 shorter events, 41.7 us)
Async XLA Ops:
  10.0 29.5 %collective-permute-start.12 = (bf16[512,256]{1,0:T(8,128)(2,1)S(1)}, bf16[512,256]{1,0:T(8,128)(2,1)S(1)}, u32[]{:S(2)}, u32[]{:S(2)}) collective-permute-start(bf16[512,256]{1,0:T(8,128)(2,1)S(1)} %shard_map.96.refs_8_.refs_0_), channel_id=1, source_target_pairs={{0,2},{1,3},{2,0},{3,1},{4,6},{5,7},{6,4},{7,5},{8,10},{9,11},{10,... | collective-permute-start | bytes 786440 | tf_op jit(solution)/shard_map/ppermute | solution.py:22
  28.3 13.6 %collective-permute-start.15 = (bf16[512,256]{1,0:T(8,128)(2,1)S(1)}, bf16[512,256]{1,0:T(8,128)(2,1)S(1)}, u32[]{:S(2)}, u32[]{:S(2)}) collective-permute-start(bf16[512,256]{1,0:T(8,128)(2,1)S(1)} %shard_map.96.refs_8_.refs_0_), channel_id=1, source_target_pairs={{0,126},{1,127},{2,124},{3,125},{4,10},{5,11},{6,8},{7,9},{8,6},{9... | collective-permute-start | bytes 786440 | tf_op jit(solution)/shard_map/ppermute | solution.py:22
  34.5 17.7 %collective-permute-start.14 = (bf16[512,256]{1,0:T(8,128)(2,1)S(1)}, bf16[512,256]{1,0:T(8,128)(2,1)S(1)}, u32[]{:S(2)}, u32[]{:S(2)}) collective-permute-start(bf16[512,256]{1,0:T(8,128)(2,1)S(1)} %shard_map.96.refs_8_.refs_0_), channel_id=1, source_target_pairs={{0,6},{1,7},{2,4},{3,5},{4,2},{5,3},{6,0},{7,1},{8,14},{9,15},{10,... | collective-permute-start | bytes 786440 | tf_op jit(solution)/shard_map/ppermute | solution.py:22
  35.4 20.9 %collective-permute-start.18 = (bf16[3,64,1024]{2,1,0:T(8,128)(2,1)}, bf16[3,64,1024]{2,1,0:T(8,128)(2,1)S(1)}, u32[]{:S(2)}, u32[]{:S(2)}) collective-permute-start(bf16[3,64,1024]{2,1,0:T(8,128)(2,1)} %get-tuple-element.48), channel_id=1, source_target_pairs={{0,0},{1,4},{2,8},{3,12},{4,1},{5,5},{6,9},{7,13},{8,2},{9,6},{10,... | collective-permute-start | bytes 1179656 | tf_op jit(solution)/shard_map/ppermute | solution.py:22
  37.1 16.5 %collective-permute-start.10 = (bf16[64,1024]{1,0:T(8,128)(2,1)}, bf16[64,1024]{1,0:T(8,128)(2,1)S(1)}, u32[]{:S(2)}, u32[]{:S(2)}) collective-permute-start(bf16[64,1024]{1,0:T(8,128)(2,1)} %bitcast.13.refs_3_), channel_id=1, source_target_pairs={{0,1},{1,0},{2,3},{3,2},{4,5},{5,4},{6,7},{7,6},{8,9},{9,8},{10,11... | collective-permute-start | bytes 393224 | tf_op jit(solution)/shard_map/ppermute | solution.py:22
  39.5 14.1 %collective-permute-start.7 = (bf16[64,1024]{1,0:T(8,128)(2,1)}, bf16[64,1024]{1,0:T(8,128)(2,1)S(1)}, u32[]{:S(2)}, u32[]{:S(2)}) collective-permute-start(bf16[64,1024]{1,0:T(8,128)(2,1)} %bitcast.10.refs_0_), channel_id=1, source_target_pairs={{0,1},{1,0},{2,3},{3,2},{4,5},{5,4},{6,7},{7,6},{8,9},{9,8},{10,11... | collective-permute-start | bytes 393224 | tf_op jit(solution)/shard_map/ppermute | solution.py:22
  41.9 22.1 %collective-permute-start.19 = (bf16[3,64,1024]{2,1,0:T(8,128)(2,1)}, bf16[3,64,1024]{2,1,0:T(8,128)(2,1)}, u32[]{:S(2)}, u32[]{:S(2)}) collective-permute-start(bf16[3,64,1024]{2,1,0:T(8,128)(2,1)} %get-tuple-element.47), channel_id=1, source_target_pairs={{0,4},{1,0},{2,12},{3,8},{4,5},{5,1},{6,13},{7,9},{8,6},{9,2},{10,... | collective-permute-start | bytes 1179656 | tf_op jit(solution)/shard_map/ppermute | solution.py:22
  52.2 19.8 %collective-permute-start.20 = (bf16[3,64,1024]{2,1,0:T(8,128)(2,1)}, bf16[3,64,1024]{2,1,0:T(8,128)(2,1)}, u32[]{:S(2)}, u32[]{:S(2)}) collective-permute-start(bf16[3,64,1024]{2,1,0:T(8,128)(2,1)} %get-tuple-element.49), channel_id=1, source_target_pairs={{0,8},{1,12},{2,0},{3,4},{4,9},{5,13},{6,1},{7,5},{8,10},{9,14},{1... | collective-permute-start | bytes 1179656 | tf_op jit(solution)/shard_map/ppermute | solution.py:22
  55.7 21.5 %collective-permute-start.26 = (f32[512,256]{1,0:T(8,128)S(1)}, f32[512,256]{1,0:T(8,128)S(1)}, u32[]{:S(2)}, u32[]{:S(2)}) collective-permute-start(f32[512,256]{1,0:T(8,128)S(1)} %copy-done.3), channel_id=1, source_target_pairs={{0,1},{1,0},{2,3},{3,2},{4,5},{5,4},{6,7},{7,6},{8,9},{9,8},{10,11... | collective-permute-start | bytes 1572872 | tf_op jit(solution)/shard_map/ppermute | solution.py:22
  55.8 22.6 %collective-permute-start.27 = (f32[512,256]{1,0:T(8,128)S(1)}, f32[512,256]{1,0:T(8,128)}, u32[]{:S(2)}, u32[]{:S(2)}) collective-permute-start(f32[512,256]{1,0:T(8,128)S(1)} %copy-done.19), channel_id=1, source_target_pairs={{0,1},{1,0},{2,3},{3,2},{4,5},{5,4},{6,7},{7,6},{8,9},{9,8},{10,11... | collective-permute-start | bytes 1572872 | tf_op jit(solution)/shard_map/ppermute | solution.py:22
  57.1 20.0 %collective-permute-start.21 = (bf16[3,64,1024]{2,1,0:T(8,128)(2,1)S(1)}, bf16[3,64,1024]{2,1,0:T(8,128)(2,1)}, u32[]{:S(2)}, u32[]{:S(2)}) collective-permute-start(bf16[3,64,1024]{2,1,0:T(8,128)(2,1)S(1)} %get-tuple-element.46), channel_id=1, source_target_pairs={{0,12},{1,8},{2,4},{3,0},{4,13},{5,9},{6,5},{7,1},{8,14},{9,10},{1... | collective-permute-start | bytes 1179656 | tf_op jit(solution)/shard_map/ppermute | solution.py:22
  58.4 20.0 %all-to-all-start.1 = ((bf16[16,64,256]{2,1,0:T(8,128)(2,1)}), bf16[16,64,256]{2,1,0:T(8,128)(2,1)S(1)}, u32[]{:S(2)}, u32[]{:S(2)}) async-start(bf16[16,64,256]{2,1,0:T(8,128)(2,1)} %bitcast.17), calls=%async_computation.1 | async-start | bytes 1048576 | tf_op jit(solution)/shard_map/all_to_all | solution.py:223
  64.0 25.5 %collective-permute-start.28 = (f32[512,256]{1,0:T(8,128)S(1)}, f32[512,256]{1,0:T(8,128)}, u32[]{:S(2)}, u32[]{:S(2)}) collective-permute-start(f32[512,256]{1,0:T(8,128)S(1)} %copy-done.20), channel_id=1, source_target_pairs={{0,1},{1,0},{2,3},{3,2},{4,5},{5,4},{6,7},{7,6},{8,9},{9,8},{10,11... | collective-permute-start | bytes 1572872 | tf_op jit(solution)/shard_map/ppermute | solution.py:22
  72.0 17.7 %collective-permute-start.29 = (f32[512,256]{1,0:T(8,128)}, f32[512,256]{1,0:T(8,128)}, u32[]{:S(2)}, u32[]{:S(2)}) collective-permute-start(f32[512,256]{1,0:T(8,128)} %refs_3_.1), channel_id=1, source_target_pairs={{0,1},{1,0},{2,3},{3,2},{4,5},{5,4},{6,7},{7,6},{8,9},{9,8},{10,11... | collective-permute-start | bytes 1572872 | tf_op jit(solution)/shard_map/ppermute | solution.py:22
  77.1 13.0 %collective-permute-start.16 = (bf16[512,256]{1,0:T(8,128)(2,1)S(1)}, bf16[512,256]{1,0:T(8,128)(2,1)S(1)}, u32[]{:S(2)}, u32[]{:S(2)}) collective-permute-start(bf16[512,256]{1,0:T(8,128)(2,1)S(1)} %collective-permute-done.12.refs_9_.refs_1_), channel_id=1, source_target_pairs={{0,6},{1,7},{2,4},{3,5},{4,2},{5,3},{6,0},{7,1},{8,14},{9,15},{10,... | collective-permute-start | bytes 786440 | tf_op jit(solution)/shard_map/ppermute | solution.py:22
  77.1 13.1 %collective-permute-start.17 = (bf16[512,256]{1,0:T(8,128)(2,1)}, bf16[512,256]{1,0:T(8,128)(2,1)}, u32[]{:S(2)}, u32[]{:S(2)}) collective-permute-start(bf16[512,256]{1,0:T(8,128)(2,1)} %copy-done.27), channel_id=1, source_target_pairs={{0,2},{1,3},{2,0},{3,1},{4,6},{5,7},{6,4},{7,5},{8,10},{9,11},{10,... | collective-permute-start | bytes 786440 | tf_op jit(solution)/shard_map/ppermute | solution.py:22
  78.4 22.2 %collective-permute-start.13 = (bf16[1024,256]{1,0:T(8,128)(2,1)S(1)}, bf16[1024,256]{1,0:T(8,128)(2,1)S(1)}, u32[]{:S(2)}, u32[]{:S(2)}) collective-permute-start(bf16[1024,256]{1,0:T(8,128)(2,1)S(1)} %bitcast.48), channel_id=1, source_target_pairs={{0,1},{1,0},{2,3},{3,2},{4,5},{5,4},{6,7},{7,6},{8,9},{9,8},{10,11... | collective-permute-start | bytes 1572872 | tf_op jit(solution)/shard_map/ppermute | solution.py:22
  81.4 22.6 %all-to-all-start = ((bf16[64,16,256]{2,1,0:T(8,128)(2,1)}), bf16[64,16,256]{2,1,0:T(8,128)(2,1)S(1)}, u32[]{:S(2)}, u32[]{:S(2)}) async-start(bf16[64,16,256]{2,1,0:T(8,128)(2,1)} %bitcast.51), calls=%async_computation | async-start | bytes 1048576 | tf_op jit(solution)/shard_map/all_to_all | solution.py:245
  109.9 24.2 %collective-permute-start.32 = (bf16[512,256]{1,0:T(8,128)(2,1)}, bf16[512,256]{1,0:T(8,128)(2,1)}, u32[]{:S(2)}, u32[]{:S(2)}) collective-permute-start(bf16[512,256]{1,0:T(8,128)(2,1)} %get-tuple-element.32.own), channel_id=1, source_target_pairs={{0,126},{1,127},{2,124},{3,125},{4,10},{5,11},{6,8},{7,9},{8,6},{9... | collective-permute-start | bytes 786440 | tf_op jit(solution)/shard_map/ppermute | solution.py:22
  119.8 33.2 %all-to-all-start.2 = ((bf16[64,16,256]{2,1,0:T(8,128)(2,1)}), bf16[64,16,256]{2,1,0:T(8,128)(2,1)}, u32[]{:S(2)}, u32[]{:S(2)}) async-start(bf16[64,16,256]{2,1,0:T(8,128)(2,1)} %bitcast.47), calls=%async_computation.2 | async-start | bytes 1048576 | tf_op jit(solution)/shard_map/all_to_all | solution.py:245
  130.8 15.5 %collective-permute-start.31 = (bf16[512,256]{1,0:T(8,128)(2,1)S(1)}, bf16[512,256]{1,0:T(8,128)(2,1)}, u32[]{:S(2)}, u32[]{:S(2)}) collective-permute-start(bf16[512,256]{1,0:T(8,128)(2,1)S(1)} %copy-done.7), channel_id=1, source_target_pairs={{0,6},{1,7},{2,4},{3,5},{4,2},{5,3},{6,0},{7,1},{8,14},{9,15},{10,... | collective-permute-start | bytes 786440 | tf_op jit(solution)/shard_map/ppermute | solution.py:22
  133.6 17.1 %collective-permute-start.33 = (bf16[512,256]{1,0:T(8,128)(2,1)}, bf16[512,256]{1,0:T(8,128)(2,1)}, u32[]{:S(2)}, u32[]{:S(2)}) collective-permute-start(bf16[512,256]{1,0:T(8,128)(2,1)} %copy-done.8), channel_id=1, source_target_pairs={{0,6},{1,7},{2,4},{3,5},{4,2},{5,3},{6,0},{7,1},{8,14},{9,15},{10,... | collective-permute-start | bytes 786440 | tf_op jit(solution)/shard_map/ppermute | solution.py:22
  134.1 16.6 %collective-permute-start.34 = (bf16[512,256]{1,0:T(8,128)(2,1)}, bf16[512,256]{1,0:T(8,128)(2,1)}, u32[]{:S(2)}, u32[]{:S(2)}) collective-permute-start(bf16[512,256]{1,0:T(8,128)(2,1)} %collective-permute-done.32.outer), channel_id=1, source_target_pairs={{0,2},{1,3},{2,0},{3,1},{4,6},{5,7},{6,4},{7,5},{8,10},{9,11},{10,... | collective-permute-start | bytes 786440 | tf_op jit(solution)/shard_map/ppermute | solution.py:22
  137.5 18.8 %collective-permute-start.36 = (f32[256,256]{1,0:T(8,128)}, f32[256,256]{1,0:T(8,128)}, u32[]{:S(2)}, u32[]{:S(2)}) collective-permute-start(f32[256,256]{1,0:T(8,128)} %get-tuple-element.45), channel_id=1, source_target_pairs={{0,1},{1,0},{2,3},{3,2},{4,5},{5,4},{6,7},{7,6},{8,9},{9,8},{10,11... | collective-permute-start | bytes 786440 | tf_op jit(solution)/shard_map/ppermute | solution.py:22
  (53 other events, 498.3 us)

commit v3 on v2

--- a/solution.py
+++ b/solution.py
@@ -34,6 +34,7 @@
 SLIP = shape(512, 256, dtype=BF16)
 TURNED = shape(256, 256)
 HALF = shape(256, 256, dtype=BF16)
+QUARTER = shape(4, 16, 1024, dtype=BF16)
 LEFT = shape(512, 1024, dtype=BF16)
 SENT = shape(32, 2, 16, 256, dtype=BF16)
 RIGHT = shape(512, 1024, dtype=BF16)
@@ -42,7 +43,7 @@
 VECTORS = pl.BlockSpec(memory_space=pltpu.VMEM)
 
 
-SMALL = ("coeff", "near", "near_outer", "raise", "join")
+SMALL = ("choose", "coeff", "near", "near_outer", "raise", "join")
 
 
 def call(kernel, outs, where, operands, name, flops, scratch=()):
@@ -114,6 +115,26 @@
 def left_kernel(where_ref, own, received, out_ref):
     out_ref[:256] = own[...].T
     out_ref[256:] = received[...].T
+
+
+def choose_kernel(where_ref, *refs):
+    for u in range(4):
+        for t in range(4):
+            @pl.when(where_ref[5] == (u ^ t))
+            def _(u=u, t=t):
+                refs[4 + u][...] = refs[t][...]
+
+
+def mask_kernel(where_ref, ranks_ref, left, out_ref):
+    level = lax.broadcasted_iota(jnp.int32, (32, 256), 0)
+    for i in range(4):
+        for j in range(2):
+            distance = jnp.abs(where_ref[6] * 4 + i - (where_ref[7] * 2 + j))
+            far = jnp.minimum(distance, 32 - distance) > 1
+            rank = jnp.where(far, ranks_ref[i, j], 0)
+            for q in range(4):
+                kept = left[i, j, :, q * 256 : q * 256 + 256].astype(F32)
+                out_ref[i * 4 + q, j * 32 : j * 32 + 32, :] = jnp.where(level < rank, kept, 0.0).astype(BF16)
 
 
 def raise_kernel(where_ref, log, own, theirs):
@@ -194,7 +215,7 @@
     col = chip * 2 + core
     block, quarter = col // 4, col % 4
     x_at, z_at = row % 4, chip % 4
-    where = jnp.stack([quarter, core, block, x_at, block % 2]).astype(jnp.int32)
+    where = jnp.stack([quarter, core, block, x_at, block % 2, z_at ^ x_at, row, col]).astype(jnp.int32)
     partner = lambda d: d ^ 1
     zl = lambda d: d ^ 2
 
@@ -206,20 +227,18 @@
         r, c = d // 16, d % 16
         return ((c // 8) * 4 + ((r % 4) ^ u)) * 16 + (c % 2) * 8 + (c // 2 % 4) * 2 + r // 4
 
-    arrived = [
-        move(lax.select_n(z_at ^ x_at ^ u, *along), functools.partial(right_target, u=u)).reshape(64, 1024)
-        for u in range(4)
-    ]
+    chosen = call(choose_kernel, [QUARTER] * 4, where, along, "choose", 1)
+    arrived = [move(chosen[u], functools.partial(right_target, u=u)).reshape(64, 1024) for u in range(4)]
     right_parts = arrived + [move(arrived[u], partner) for u in range(4)]
 
-    levels = jnp.arange(32, dtype=jnp.int32)
-    rows_of = row * 4 + jnp.arange(4, dtype=jnp.int32)
-    cols_of = col * 2 + jnp.arange(2, dtype=jnp.int32)
-    distance = jnp.abs(rows_of[:, None] - cols_of[None, :])
-    far = jnp.minimum(distance, 32 - distance) > 1
-    keep = ((levels < block_ranks[:, :, None]) & far[:, :, None]).reshape(4, 1, 64, 1)
-    left_out = low_left.reshape(4, 64, 4, 256).transpose(0, 2, 1, 3)
-    left_out = jnp.where(keep, left_out, 0).astype(BF16).reshape(16, 64, 256)
+    left_out = pl.pallas_call(
+        mask_kernel,
+        out_shape=shape(16, 64, 256, dtype=BF16),
+        in_specs=[SCALARS, SCALARS, VECTORS],
+        out_specs=VECTORS,
+        compiler_params=pltpu.CompilerParams(vmem_limit_bytes=20 << 20),
+        name="mask",
+    )(where, block_ranks, low_left)
     left = lax.all_to_all(left_out, ("chip", "core"), 0, 0).reshape(1024, 256)
     lefts = (left, move(left, partner))
 

time: 161 us -> 161 us (level)
  starting transfers between devices: 66.7 us -> 87.2 us
  waiting for transfers between devices: 43.9 us -> 27.6 us
  local copies, waits for them, and re-layouts: 14.6 us -> 11.2 us
  other arithmetic: 2.34 us -> 0 us
  Pallas kernels: 30.1 us -> 32.2 us
    ppermute x37, waiting for transfers between devices: 42.7 us -> 20.7 us  [move(): return lax.ppermute(value, ALL, [(d, target(d)) for d in range(COUNT)])]
    ppermute x37, starting transfers between devices: 42.2 us -> 63.9 us  [move(): return lax.ppermute(value, ALL, [(d, target(d)) for d in range(COUNT)])]
    all_to_all x1, waiting for transfers between devices: 1.17 us -> 6.88 us  [on_device(): left = lax.all_to_all(left_out, ('chip', 'core'), 0, 0).reshape(1024, 256)]
    select_n x2 -> x0, other arithmetic: 2.25 us -> none  [the longest x1 1.78 us: on_device(): lax.select_n(z_at ^ x_at ^ u, *along)]
    all_to_all x1, starting transfers between devices: 5.54 us -> 3.57 us  [on_device(): left = lax.all_to_all(left_out, ('chip', 'core'), 0, 0).reshape(1024, 256)]
    unnamed x75 -> x83, local copies, waits for them, and re-layouts: 8 us -> 7.1 us
    pallas_call x12 -> x13, Pallas kernels: 30.1 us -> 30.8 us  [call(): pl.pallas_call(kernel, out_shape=outs, in_specs=[SCALARS] + [VECTORS] * l...]
  transfers between devices with their start and end apart: 40 -> 40, of which waited for: 11 -> 10; matrix products, arithmetic and copies ran while one was open for 5% -> 1% of each run, Pallas kernels for 16% -> 18%
where the time goes in v3:
time: 161 us; the launch traced here: 159 us
  starting transfers between devices  87.2 us (54%)
  Pallas kernels  32.2 us (20%)
  waiting for transfers between devices  27.6 us (17%)
  local copies, waits for them, and re-layouts  11.2 us (7%)
    ppermute x37, starting transfers between devices, move(): return lax.ppermute(value, ALL, [(d, target(d)) for d in range(COUNT)])  63.9 us
    pallas_call x13, Pallas kernels, call(): pl.pallas_call(kernel, out_shape=outs, in_specs=[SCALARS] + [VECTORS] * l...  30.8 us
    ppermute x37, waiting for transfers between devices, move(): return lax.ppermute(value, ALL, [(d, target(d)) for d in range(COUNT)])  20.7 us
    all_to_all x2, starting transfers between devices, all_to_all(): lax.all_to_all(sent.reshape(64, 16, 256), ('row', 'chip'), 0, 0)  19.7 us
    unnamed x83, local copies, waits for them, and re-layouts  7.1 us
    all_to_all x1, waiting for transfers between devices, on_device(): left = lax.all_to_all(left_out, ('chip', 'core'), 0, 0).reshape(1024, 256)  6.88 us
    all_to_all x1, starting transfers between devices, on_device(): left = lax.all_to_all(left_out, ('chip', 'core'), 0, 0).reshape(1024, 256)  3.57 us
  transfers between devices with their start and end apart: 40, of which 10 were waited for; matrix products, arithmetic and copies ran while one was open for 1% of the time, Pallas kernels for 18%

profile of v3, /device:TPU:0, one launch (start us, length us, event | category | flops | bytes accessed | tf_op | source)
XLA Modules:
  0.0 159.3 jit_solution(17293706849160494994)
XLA Ops:
  2.0 2.1 %collective-permute-start = (bf16[4,16,1024]{2,1,0:T(8,128)(2,1)S(1)}, bf16[4,16,1024]{2,1,0:T(8,128)(2,1)S(1)}, u32[]{:S(2)}, u32[]{:S(2)}) collective-permute-start(bf16[4,16,1024]{2,1,0:T(8,128)(2,1)S(1)} %get-tuple-element.60), channel_id=1, source_target_pairs={{0,2},{1,3},{2,0},{3,1},{4,6},{5,7},{6,4},{7,5},{8,10},{9,11},{10,... | collective-permute-start | bytes 393224 | tf_op jit(solution)/shard_map/ppermute | solution.py:22
  4.1 3.6 %collective-permute-start.1 = (bf16[4,16,1024]{2,1,0:T(8,128)(2,1)S(1)}, bf16[4,16,1024]{2,1,0:T(8,128)(2,1)S(1)}, u32[]{:S(2)}, u32[]{:S(2)}) collective-permute-start(bf16[4,16,1024]{2,1,0:T(8,128)(2,1)S(1)} %get-tuple-element.59), channel_id=1, source_target_pairs={{0,4},{1,5},{2,6},{3,7},{4,0},{5,1},{6,2},{7,3},{8,12},{9,13},{10,... | collective-permute-start | bytes 393224 | tf_op jit(solution)/shard_map/ppermute | solution.py:22
  8.5 5.3 %collective-permute-done.1.refs_2_ = bf16[4,16,1024]{2,1,0:T(8,128)(2,1)S(1)} collective-permute-done((bf16[4,16,1024]{2,1,0:T(8,128)(2,1)S(1)}, bf16[4,16,1024]{2,1,0:T(8,128)(2,1)S(1)}, u32[]{:S(2)}, u32[]{:S(2)}) %collective-permute-start.1) | collective-permute-done | bytes 131104 | tf_op jit(solution)/shard_map/ppermute | solution.py:22
  13.8 2.1 %collective-permute-done.2.refs_3_ = bf16[4,16,1024]{2,1,0:T(8,128)(2,1)S(1)} collective-permute-done((bf16[4,16,1024]{2,1,0:T(8,128)(2,1)S(1)}, bf16[4,16,1024]{2,1,0:T(8,128)(2,1)S(1)}, u32[]{:S(2)}, u32[]{:S(2)}) %collective-permute-start.2) | collective-permute-done | bytes 131104 | tf_op jit(solution)/shard_map/ppermute | solution.py:22
  16.6 2.8 %collective-permute-start.6 = (bf16[4,16,1024]{2,1,0:T(8,128)(2,1)S(1)}, bf16[4,16,1024]{2,1,0:T(8,128)(2,1)S(1)}, u32[]{:S(2)}, u32[]{:S(2)}) collective-permute-start(bf16[4,16,1024]{2,1,0:T(8,128)(2,1)S(1)} %get-tuple-element.31), channel_id=1, source_target_pairs={{0,48},{1,56},{2,50},{3,58},{4,52},{5,60},{6,54},{7,62},{8,112},{9... | collective-permute-start | bytes 393224 | tf_op jit(solution)/shard_map/ppermute | solution.py:22
  21.1 6.2 %collective-permute-start.15 = (bf16[512,256]{1,0:T(8,128)(2,1)S(1)}, bf16[512,256]{1,0:T(8,128)(2,1)}, u32[]{:S(2)}, u32[]{:S(2)}) collective-permute-start(bf16[512,256]{1,0:T(8,128)(2,1)S(1)} %shard_map.97.refs_8_.refs_0_), channel_id=1, source_target_pairs={{0,126},{1,127},{2,124},{3,125},{4,10},{5,11},{6,8},{7,9},{8,6},{9... | collective-permute-start | bytes 786440 | tf_op jit(solution)/shard_map/ppermute | solution.py:22
  31.2 3.1 %collective-permute-start.10 = (bf16[64,1024]{1,0:T(8,128)(2,1)S(1)}, bf16[64,1024]{1,0:T(8,128)(2,1)S(1)}, u32[]{:S(2)}, u32[]{:S(2)}) collective-permute-start(bf16[64,1024]{1,0:T(8,128)(2,1)S(1)} %bitcast.48), channel_id=1, source_target_pairs={{0,1},{1,0},{2,3},{3,2},{4,5},{5,4},{6,7},{7,6},{8,9},{9,8},{10,11... | collective-permute-start | bytes 393224 | tf_op jit(solution)/shard_map/ppermute | solution.py:22
  36.9 9.4 %collective-permute-start.19 = (bf16[3,64,1024]{2,1,0:T(8,128)(2,1)}, bf16[3,64,1024]{2,1,0:T(8,128)(2,1)}, u32[]{:S(2)}, u32[]{:S(2)}) collective-permute-start(bf16[3,64,1024]{2,1,0:T(8,128)(2,1)} %get-tuple-element.55), channel_id=1, source_target_pairs={{0,4},{1,0},{2,12},{3,8},{4,5},{5,1},{6,13},{7,9},{8,6},{9,2},{10,... | collective-permute-start | bytes 1179656 | tf_op jit(solution)/shard_map/ppermute | solution.py:22
  49.1 12.9 %collective-permute-start.27 = (f32[512,256]{1,0:T(8,128)}, f32[512,256]{1,0:T(8,128)}, u32[]{:S(2)}, u32[]{:S(2)}) collective-permute-start(f32[512,256]{1,0:T(8,128)} %refs_1_.1), channel_id=1, source_target_pairs={{0,1},{1,0},{2,3},{3,2},{4,5},{5,4},{6,7},{7,6},{8,9},{9,8},{10,11... | collective-permute-start | bytes 1572872 | tf_op jit(solution)/shard_map/ppermute | solution.py:22
  63.5 3.6 %all-to-all-start.1 = ((bf16[16,64,256]{2,1,0:T(8,128)(2,1)}), bf16[16,64,256]{2,1,0:T(8,128)(2,1)S(1)}, u32[]{:S(2)}, u32[]{:S(2)}) async-start(bf16[16,64,256]{2,1,0:T(8,128)(2,1)} %mask.1), calls=%async_computation.1 | async-start | bytes 1048576 | tf_op jit(solution)/shard_map/all_to_all | solution.py:242
  67.7 3.0 %collective-permute-start.16 = (bf16[512,256]{1,0:T(8,128)(2,1)S(1)}, bf16[512,256]{1,0:T(8,128)(2,1)}, u32[]{:S(2)}, u32[]{:S(2)}) collective-permute-start(bf16[512,256]{1,0:T(8,128)(2,1)S(1)} %collective-permute-done.12.refs_9_.refs_1_), channel_id=1, source_target_pairs={{0,6},{1,7},{2,4},{3,5},{4,2},{5,3},{6,0},{7,1},{8,14},{9,15},{10,... | collective-permute-start | bytes 786440 | tf_op jit(solution)/shard_map/ppermute | solution.py:22
  71.0 6.9 %all-to-all-done.1 = bf16[16,64,256]{2,1,0:T(8,128)(2,1)S(1)} async-done(((bf16[16,64,256]{2,1,0:T(8,128)(2,1)}), bf16[16,64,256]{2,1,0:T(8,128)(2,1)S(1)}, u32[]{:S(2)}, u32[]{:S(2)}) %all-to-all-start.1) | async-done | bytes 524320 | tf_op jit(solution)/shard_map/all_to_all | solution.py:242
  77.9 3.0 %shard_map.98 = (bf16[32,2,16,256]{3,2,1,0:T(8,128)(2,1)}, bf16[512,1024]{1,0:T(8,128)(2,1)}) custom-call(s32[8]{0:T(128)} %copy-done.12, bf16[64,1024]{1,0:T(8,128)(2,1)} %bitcast.50, bf16[64,1024]{1,0:T(8,128)(2,1)} %bitcast.52, bf16[64,1024]{1,0:T(8,128)(2,1)} %bitcast.55, bf16[64,1024]{1,0:T(8,128)(2,1)} %bitcast.49, bf16[64,1024]{1,0:T(8,128)(2,1)} %copy-done.35, ...), custom_call_target="tpu_custom_call" | custom-call | flops 268435456 | bytes 5242880 | tf_op jit(solution)/shard_map/pallas_call | solution.py:50
  80.9 8.8 %all-to-all-start = ((bf16[64,16,256]{2,1,0:T(8,128)(2,1)}), bf16[64,16,256]{2,1,0:T(8,128)(2,1)S(1)}, u32[]{:S(2)}, u32[]{:S(2)}) async-start(bf16[64,16,256]{2,1,0:T(8,128)(2,1)} %bitcast.47), calls=%async_computation | async-start | bytes 1048576 | tf_op jit(solution)/shard_map/all_to_all | solution.py:264
  90.8 4.4 %shard_map.100 = (f32[512,256]{1,0:T(8,128)}, f32[512,256]{1,0:T(8,128)}, f32[512,256]{1,0:T(8,128)}, f32[512,256]{1,0:T(8,128)}, f32[512,256]{1,0:T(8,128)}, /*index=5*/f32[512,256]{1,0:T(8,128)}, f32[512,256]{1,0:T(8,128)}) custom-call(s32[8]{0:T(128)} %copy-done.12, f32[512,256]{1,0:T(8,128)} %refs_0_.1, f32[512,256]{1,0:T(8,128)} %refs_1_.1, ...), custom_call_target="tpu_custom_call" | custom-call | flops 1 | bytes 5242880 | tf_op jit(solution)/shard_map/pallas_call | solution.py:50
  96.4 4.7 %shard_map.101 = (f32[512,256]{1,0:T(8,128)}, bf16[3,512,1024]{2,1,0:T(8,128)(2,1)}) custom-call(s32[8]{0:T(128)} %copy-done.12, bf16[512,256]{1,0:T(8,128)(2,1)} %copy-done.1, bf16[512,256]{1,0:T(8,128)(2,1)} %copy-done.18, bf16[512,256]{1,0:T(8,128)(2,1)} %collective-permute-done.14.refs_2_, bf16[512,256]{1,0:T(8,128)(2,1)} %collective-permute-done.15.refs_3_, ...), custom_call_target="tpu_custom_call" | custom-call | flops 805306368 | bytes 5242880 | tf_op jit(solution)/shard_map/pallas_call | solution.py:50
  101.9 2.6 %shard_map.99.left = bf16[512,1024]{1,0:T(8,128)(2,1)} custom-call(s32[8]{0:T(128)} %copy-done.12, bf16[1024,256]{1,0:T(8,128)(2,1)} %bitcast.44, bf16[1024,256]{1,0:T(8,128)(2,1)} %copy-done.22), custom_call_target="tpu_custom_call" | custom-call | flops 1048576 | bytes 5242880 | tf_op jit(solution)/shard_map/pallas_call | solution.py:50
  105.3 3.5 %shard_map.102 = (f32[512,256]{1,0:T(8,128)}, f32[512,256]{1,0:T(8,128)}, bf16[512,256]{1,0:T(8,128)(2,1)}) custom-call(s32[8]{0:T(128)} %copy-done.12, bf16[1024,256]{1,0:T(8,128)(2,1)} %bitcast.45, bf16[512,1024]{1,0:T(8,128)(2,1)} %shard_map.99.left, f32[512,256]{1,0:T(8,128)} %get-tuple-element.37.num, f32[512,256]{1,0:T(8,128)} %get-tuple-element.38.den, ...), custom_call_target="tpu_custom_call" | custom-call | flops 268435456 | bytes 5242880 | tf_op jit(solution)/shard_map/pallas_call | solution.py:50
  110.4 6.6 %collective-permute-start.32 = (bf16[512,256]{1,0:T(8,128)(2,1)}, bf16[512,256]{1,0:T(8,128)(2,1)}, u32[]{:S(2)}, u32[]{:S(2)}) collective-permute-start(bf16[512,256]{1,0:T(8,128)(2,1)} %get-tuple-element.40.own), channel_id=1, source_target_pairs={{0,126},{1,127},{2,124},{3,125},{4,10},{5,11},{6,8},{7,9},{8,6},{9... | collective-permute-start | bytes 786440 | tf_op jit(solution)/shard_map/ppermute | solution.py:22
  120.4 10.9 %all-to-all-start.2 = ((bf16[64,16,256]{2,1,0:T(8,128)(2,1)}), bf16[64,16,256]{2,1,0:T(8,128)(2,1)}, u32[]{:S(2)}, u32[]{:S(2)}) async-start(bf16[64,16,256]{2,1,0:T(8,128)(2,1)} %bitcast.42), calls=%async_computation.2 | async-start | bytes 1048576 | tf_op jit(solution)/shard_map/all_to_all | solution.py:264
  131.3 2.8 %collective-permute-start.31 = (bf16[512,256]{1,0:T(8,128)(2,1)S(1)}, bf16[512,256]{1,0:T(8,128)(2,1)}, u32[]{:S(2)}, u32[]{:S(2)}) collective-permute-start(bf16[512,256]{1,0:T(8,128)(2,1)S(1)} %copy-done.6), channel_id=1, source_target_pairs={{0,6},{1,7},{2,4},{3,5},{4,2},{5,3},{6,0},{7,1},{8,14},{9,15},{10,... | collective-permute-start | bytes 786440 | tf_op jit(solution)/shard_map/ppermute | solution.py:22
  134.9 3.1 %shard_map.104 = (f32[512,256]{1,0:T(8,128)}, f32[512,256]{1,0:T(8,128)}, f32[512,256]{1,0:T(8,128)}, f32[256,256]{1,0:T(8,128)}) custom-call(s32[8]{0:T(128)} %copy-done.12, f32[512,256]{1,0:T(8,128)} %get-tuple-element.41.log, f32[512,256]{1,0:T(8,128)} %get-tuple-element.42.state, f32[512,256]{1,0:T(8,128)} %get-tuple-element.43.effect, ...), custom_call_target="tpu_custom_call" | custom-call | flops 1 | bytes 5242880 | tf_op jit(solution)/shard_map/pallas_call | solution.py:50
  138.0 8.8 %collective-permute-done.31.inner = bf16[512,256]{1,0:T(8,128)(2,1)} collective-permute-done((bf16[512,256]{1,0:T(8,128)(2,1)S(1)}, bf16[512,256]{1,0:T(8,128)(2,1)}, u32[]{:S(2)}, u32[]{:S(2)}) %collective-permute-start.31) | collective-permute-done | bytes 262176 | tf_op jit(solution)/shard_map/ppermute | solution.py:22
  153.5 3.3 %shard_map.107 = (f32[512,256]{1,0:T(8,128)}, f32[256,256]{1,0:T(8,128)}) custom-call(s32[8]{0:T(128)} %copy-done.12, bf16[1024,256]{1,0:T(8,128)(2,1)} %bitcast.25.coeff, bf16[512,1024]{1,0:T(8,128)(2,1)} %shard_map.99.left, f32[512,256]{1,0:T(8,128)} %copy-done.4, f32[512,256]{1,0:T(8,128)} %get-tuple-element.48.den, f32[512,256]{1,0:T(8,128)} %get-tuple-element.49.sum_log), custom_call_target="tpu_custom_call" | custom-call | flops 268435456 | bytes 5242880 | tf_op jit(solution)/shard_map/pallas_call | solution.py:50
  (158 shorter events, 34.7 us)
Async XLA Ops:
  8.4 12.0 %collective-permute-start.11 = (bf16[256,256]{1,0:T(8,128)(2,1)S(1)}, bf16[256,256]{1,0:T(8,128)(2,1)S(1)}, u32[]{:S(2)}, u32[]{:S(2)}) collective-permute-start(bf16[256,256]{1,0:T(8,128)(2,1)S(1)} %get-tuple-element.33), channel_id=1, source_target_pairs={{0,1},{1,0},{2,3},{3,2},{4,5},{5,4},{6,7},{7,6},{8,9},{9,8},{10,11... | collective-permute-start | bytes 393224 | tf_op jit(solution)/shard_map/ppermute | solution.py:22
  21.0 15.9 %collective-permute-start.12 = (bf16[512,256]{1,0:T(8,128)(2,1)S(1)}, bf16[512,256]{1,0:T(8,128)(2,1)S(1)}, u32[]{:S(2)}, u32[]{:S(2)}) collective-permute-start(bf16[512,256]{1,0:T(8,128)(2,1)S(1)} %shard_map.97.refs_8_.refs_0_), channel_id=1, source_target_pairs={{0,2},{1,3},{2,0},{3,1},{4,6},{5,7},{6,4},{7,5},{8,10},{9,11},{10,... | collective-permute-start | bytes 786440 | tf_op jit(solution)/shard_map/ppermute | solution.py:22
  21.1 25.2 %collective-permute-start.15 = (bf16[512,256]{1,0:T(8,128)(2,1)S(1)}, bf16[512,256]{1,0:T(8,128)(2,1)}, u32[]{:S(2)}, u32[]{:S(2)}) collective-permute-start(bf16[512,256]{1,0:T(8,128)(2,1)S(1)} %shard_map.97.refs_8_.refs_0_), channel_id=1, source_target_pairs={{0,126},{1,127},{2,124},{3,125},{4,10},{5,11},{6,8},{7,9},{8,6},{9... | collective-permute-start | bytes 786440 | tf_op jit(solution)/shard_map/ppermute | solution.py:22
  27.3 19.0 %collective-permute-start.14 = (bf16[512,256]{1,0:T(8,128)(2,1)S(1)}, bf16[512,256]{1,0:T(8,128)(2,1)}, u32[]{:S(2)}, u32[]{:S(2)}) collective-permute-start(bf16[512,256]{1,0:T(8,128)(2,1)S(1)} %shard_map.97.refs_8_.refs_0_), channel_id=1, source_target_pairs={{0,6},{1,7},{2,4},{3,5},{4,2},{5,3},{6,0},{7,1},{8,14},{9,15},{10,... | collective-permute-start | bytes 786440 | tf_op jit(solution)/shard_map/ppermute | solution.py:22
  31.2 16.0 %collective-permute-start.10 = (bf16[64,1024]{1,0:T(8,128)(2,1)S(1)}, bf16[64,1024]{1,0:T(8,128)(2,1)S(1)}, u32[]{:S(2)}, u32[]{:S(2)}) collective-permute-start(bf16[64,1024]{1,0:T(8,128)(2,1)S(1)} %bitcast.48), channel_id=1, source_target_pairs={{0,1},{1,0},{2,3},{3,2},{4,5},{5,4},{6,7},{7,6},{8,9},{9,8},{10,11... | collective-permute-start | bytes 393224 | tf_op jit(solution)/shard_map/ppermute | solution.py:22
  35.3 13.7 %collective-permute-start.18 = (bf16[3,64,1024]{2,1,0:T(8,128)(2,1)S(1)}, bf16[3,64,1024]{2,1,0:T(8,128)(2,1)}, u32[]{:S(2)}, u32[]{:S(2)}) collective-permute-start(bf16[3,64,1024]{2,1,0:T(8,128)(2,1)S(1)} %get-tuple-element.56), channel_id=1, source_target_pairs={{0,0},{1,4},{2,8},{3,12},{4,1},{5,5},{6,9},{7,13},{8,2},{9,6},{10,... | collective-permute-start | bytes 1179656 | tf_op jit(solution)/shard_map/ppermute | solution.py:22
  36.9 30.2 %collective-permute-start.19 = (bf16[3,64,1024]{2,1,0:T(8,128)(2,1)}, bf16[3,64,1024]{2,1,0:T(8,128)(2,1)}, u32[]{:S(2)}, u32[]{:S(2)}) collective-permute-start(bf16[3,64,1024]{2,1,0:T(8,128)(2,1)} %get-tuple-element.55), channel_id=1, source_target_pairs={{0,4},{1,0},{2,12},{3,8},{4,5},{5,1},{6,13},{7,9},{8,6},{9,2},{10,... | collective-permute-start | bytes 1179656 | tf_op jit(solution)/shard_map/ppermute | solution.py:22
  46.4 21.1 %collective-permute-start.20 = (bf16[3,64,1024]{2,1,0:T(8,128)(2,1)}, bf16[3,64,1024]{2,1,0:T(8,128)(2,1)}, u32[]{:S(2)}, u32[]{:S(2)}) collective-permute-start(bf16[3,64,1024]{2,1,0:T(8,128)(2,1)} %get-tuple-element.57), channel_id=1, source_target_pairs={{0,8},{1,12},{2,0},{3,4},{4,9},{5,13},{6,1},{7,5},{8,10},{9,14},{1... | collective-permute-start | bytes 1179656 | tf_op jit(solution)/shard_map/ppermute | solution.py:22
  48.6 22.2 %collective-permute-start.26 = (f32[512,256]{1,0:T(8,128)S(1)}, f32[512,256]{1,0:T(8,128)S(1)}, u32[]{:S(2)}, u32[]{:S(2)}) collective-permute-start(f32[512,256]{1,0:T(8,128)S(1)} %copy-done.2), channel_id=1, source_target_pairs={{0,1},{1,0},{2,3},{3,2},{4,5},{5,4},{6,7},{7,6},{8,9},{9,8},{10,11... | collective-permute-start | bytes 1572872 | tf_op jit(solution)/shard_map/ppermute | solution.py:22
  49.1 18.7 %collective-permute-start.21 = (bf16[3,64,1024]{2,1,0:T(8,128)(2,1)}, bf16[3,64,1024]{2,1,0:T(8,128)(2,1)}, u32[]{:S(2)}, u32[]{:S(2)}) collective-permute-start(bf16[3,64,1024]{2,1,0:T(8,128)(2,1)} %get-tuple-element.54), channel_id=1, source_target_pairs={{0,12},{1,8},{2,4},{3,0},{4,13},{5,9},{6,5},{7,1},{8,14},{9,10},{1... | collective-permute-start | bytes 1179656 | tf_op jit(solution)/shard_map/ppermute | solution.py:22
  49.1 28.8 %collective-permute-start.27 = (f32[512,256]{1,0:T(8,128)}, f32[512,256]{1,0:T(8,128)}, u32[]{:S(2)}, u32[]{:S(2)}) collective-permute-start(f32[512,256]{1,0:T(8,128)} %refs_1_.1), channel_id=1, source_target_pairs={{0,1},{1,0},{2,3},{3,2},{4,5},{5,4},{6,7},{7,6},{8,9},{9,8},{10,11... | collective-permute-start | bytes 1572872 | tf_op jit(solution)/shard_map/ppermute | solution.py:22
  63.5 14.4 %all-to-all-start.1 = ((bf16[16,64,256]{2,1,0:T(8,128)(2,1)}), bf16[16,64,256]{2,1,0:T(8,128)(2,1)S(1)}, u32[]{:S(2)}, u32[]{:S(2)}) async-start(bf16[16,64,256]{2,1,0:T(8,128)(2,1)} %mask.1), calls=%async_computation.1 | async-start | bytes 1048576 | tf_op jit(solution)/shard_map/all_to_all | solution.py:242
  67.1 22.6 %collective-permute-start.28 = (f32[512,256]{1,0:T(8,128)S(1)}, f32[512,256]{1,0:T(8,128)}, u32[]{:S(2)}, u32[]{:S(2)}) collective-permute-start(f32[512,256]{1,0:T(8,128)S(1)} %copy-done.19), channel_id=1, source_target_pairs={{0,1},{1,0},{2,3},{3,2},{4,5},{5,4},{6,7},{7,6},{8,9},{9,8},{10,11... | collective-permute-start | bytes 1572872 | tf_op jit(solution)/shard_map/ppermute | solution.py:22
  67.5 22.3 %collective-permute-start.29 = (f32[512,256]{1,0:T(8,128)S(1)}, f32[512,256]{1,0:T(8,128)}, u32[]{:S(2)}, u32[]{:S(2)}) collective-permute-start(f32[512,256]{1,0:T(8,128)S(1)} %copy-done.20), channel_id=1, source_target_pairs={{0,1},{1,0},{2,3},{3,2},{4,5},{5,4},{6,7},{7,6},{8,9},{9,8},{10,11... | collective-permute-start | bytes 1572872 | tf_op jit(solution)/shard_map/ppermute | solution.py:22
  67.7 22.6 %collective-permute-start.16 = (bf16[512,256]{1,0:T(8,128)(2,1)S(1)}, bf16[512,256]{1,0:T(8,128)(2,1)}, u32[]{:S(2)}, u32[]{:S(2)}) collective-permute-start(bf16[512,256]{1,0:T(8,128)(2,1)S(1)} %collective-permute-done.12.refs_9_.refs_1_), channel_id=1, source_target_pairs={{0,6},{1,7},{2,4},{3,5},{4,2},{5,3},{6,0},{7,1},{8,14},{9,15},{10,... | collective-permute-start | bytes 786440 | tf_op jit(solution)/shard_map/ppermute | solution.py:22
  70.8 19.6 %collective-permute-start.17 = (bf16[512,256]{1,0:T(8,128)(2,1)}, bf16[512,256]{1,0:T(8,128)(2,1)S(1)}, u32[]{:S(2)}, u32[]{:S(2)}) collective-permute-start(bf16[512,256]{1,0:T(8,128)(2,1)} %collective-permute-done.15.refs_3_), channel_id=1, source_target_pairs={{0,2},{1,3},{2,0},{3,1},{4,6},{5,7},{6,4},{7,5},{8,10},{9,11},{10,... | collective-permute-start | bytes 786440 | tf_op jit(solution)/shard_map/ppermute | solution.py:22
  77.9 23.2 %collective-permute-start.13 = (bf16[1024,256]{1,0:T(8,128)(2,1)S(1)}, bf16[1024,256]{1,0:T(8,128)(2,1)S(1)}, u32[]{:S(2)}, u32[]{:S(2)}) collective-permute-start(bf16[1024,256]{1,0:T(8,128)(2,1)S(1)} %bitcast.43), channel_id=1, source_target_pairs={{0,1},{1,0},{2,3},{3,2},{4,5},{5,4},{6,7},{7,6},{8,9},{9,8},{10,11... | collective-permute-start | bytes 1572872 | tf_op jit(solution)/shard_map/ppermute | solution.py:22
  80.9 23.6 %all-to-all-start = ((bf16[64,16,256]{2,1,0:T(8,128)(2,1)}), bf16[64,16,256]{2,1,0:T(8,128)(2,1)S(1)}, u32[]{:S(2)}, u32[]{:S(2)}) async-start(bf16[64,16,256]{2,1,0:T(8,128)(2,1)} %bitcast.47), calls=%async_computation | async-start | bytes 1048576 | tf_op jit(solution)/shard_map/all_to_all | solution.py:264
  110.4 24.2 %collective-permute-start.32 = (bf16[512,256]{1,0:T(8,128)(2,1)}, bf16[512,256]{1,0:T(8,128)(2,1)}, u32[]{:S(2)}, u32[]{:S(2)}) collective-permute-start(bf16[512,256]{1,0:T(8,128)(2,1)} %get-tuple-element.40.own), channel_id=1, source_target_pairs={{0,126},{1,127},{2,124},{3,125},{4,10},{5,11},{6,8},{7,9},{8,6},{9... | collective-permute-start | bytes 786440 | tf_op jit(solution)/shard_map/ppermute | solution.py:22
  120.4 33.1 %all-to-all-start.2 = ((bf16[64,16,256]{2,1,0:T(8,128)(2,1)}), bf16[64,16,256]{2,1,0:T(8,128)(2,1)}, u32[]{:S(2)}, u32[]{:S(2)}) async-start(bf16[64,16,256]{2,1,0:T(8,128)(2,1)} %bitcast.42), calls=%async_computation.2 | async-start | bytes 1048576 | tf_op jit(solution)/shard_map/all_to_all | solution.py:264
  131.3 15.5 %collective-permute-start.31 = (bf16[512,256]{1,0:T(8,128)(2,1)S(1)}, bf16[512,256]{1,0:T(8,128)(2,1)}, u32[]{:S(2)}, u32[]{:S(2)}) collective-permute-start(bf16[512,256]{1,0:T(8,128)(2,1)S(1)} %copy-done.6), channel_id=1, source_target_pairs={{0,6},{1,7},{2,4},{3,5},{4,2},{5,3},{6,0},{7,1},{8,14},{9,15},{10,... | collective-permute-start | bytes 786440 | tf_op jit(solution)/shard_map/ppermute | solution.py:22
  134.1 17.1 %collective-permute-start.33 = (bf16[512,256]{1,0:T(8,128)(2,1)}, bf16[512,256]{1,0:T(8,128)(2,1)}, u32[]{:S(2)}, u32[]{:S(2)}) collective-permute-start(bf16[512,256]{1,0:T(8,128)(2,1)} %copy-done.7), channel_id=1, source_target_pairs={{0,6},{1,7},{2,4},{3,5},{4,2},{5,3},{6,0},{7,1},{8,14},{9,15},{10,... | collective-permute-start | bytes 786440 | tf_op jit(solution)/shard_map/ppermute | solution.py:22
  134.6 16.6 %collective-permute-start.34 = (bf16[512,256]{1,0:T(8,128)(2,1)}, bf16[512,256]{1,0:T(8,128)(2,1)}, u32[]{:S(2)}, u32[]{:S(2)}) collective-permute-start(bf16[512,256]{1,0:T(8,128)(2,1)} %collective-permute-done.32.outer), channel_id=1, source_target_pairs={{0,2},{1,3},{2,0},{3,1},{4,6},{5,7},{6,4},{7,5},{8,10},{9,11},{10,... | collective-permute-start | bytes 786440 | tf_op jit(solution)/shard_map/ppermute | solution.py:22
  138.0 18.8 %collective-permute-start.36 = (f32[256,256]{1,0:T(8,128)}, f32[256,256]{1,0:T(8,128)}, u32[]{:S(2)}, u32[]{:S(2)}) collective-permute-start(f32[256,256]{1,0:T(8,128)} %get-tuple-element.53), channel_id=1, source_target_pairs={{0,1},{1,0},{2,3},{3,2},{4,5},{5,4},{6,7},{7,6},{8,9},{9,8},{10,11... | collective-permute-start | bytes 786440 | tf_op jit(solution)/shard_map/ppermute | solution.py:22
  (57 other events, 649.3 us)
